TPU v7x, 512 devices: a whole 4x8x8 slice. The times are simulated.
512 devices in a mesh: ep: 128 (over y, z, core), tp: 4 (over x).
Axes of the slice: x: 4, y: 8, z: 8, core: 2. Of those that a mesh axis runs over, the one named last changes fastest.
Arguments:
- queries: bfloat16 [8192, 2048], P('ep', 'tp'), may hold values from -1024 to 1024
- new_keys: bfloat16 [8192, 512], P('ep', 'tp'), may hold values from -6 to 6
- new_values: bfloat16 [8192, 512], P('ep', 'tp'), may hold values from -5 to 5
- key_cache: bfloat16 [128, 512, 512], P('ep', None, 'tp'), may hold values from -5 to 5
- value_cache: bfloat16 [128, 512, 512], P('ep', None, 'tp'), may hold values from -5 to 5
- cache_lengths: int32 [128], P('ep'), may hold values from 1 to 512, 32768 in all
- request_order: int32 [128], replicated, may hold values from 0 to 127, each once
- residual: bfloat16 [8192, 2048], P('ep', 'tp'), may hold values from -6 to 6
- out_weight: bfloat16 [2048, 2048], P('tp'), may hold values from -0.125 to 0.125
- norm_gain: float32 [2048], replicated, may hold values from 0.1 to 1.9
- route_experts: int32 [8192, 8], P('ep'), may hold values from 0 to 127, all different within a row; in each aligned block of 64 rows (0 to 63, 64 to 127, ...) at most 8 rows name the same one
- route_weights: float32 [8192, 8], P('ep'), may hold values from 0.1 to 1
- expert_gate: bfloat16 [128, 2048, 768], P('ep', None, 'tp'), may hold values from -0.125 to 0.125
- expert_up: bfloat16 [128, 2048, 768], P('ep', None, 'tp'), may hold values from -0.125 to 0.125
- expert_down: bfloat16 [128, 768, 2048], P('ep', None, 'tp'), may hold values from -0.21875 to 0.21875
Outputs:
- output: bfloat16 [8192, 2048], P('ep', 'tp')
Inputs may be any that keep to these rules, and one draw needn't show every extreme that they name: `cache_lengths`: the longest cache holds exactly 512 rows in every draw. `request_order`: each request block appears once. `route_experts`: each row names 8 different experts; within each request's block of 64 rows no expert is named by more than 8 rows, a bound that some block reaches.
All inputs are finite; a program needn't handle non-finite values. No bound on the sum of `cache_lengths` on one device may be relied on, other than what follows from the above.
Results may differ from a plain program's by a relative error of at most 0.0057.
Values may be sent and summed in bfloat16 or wider, within the bound.
A program may use at most 64 MiB of HBM per device.

v0:
```python
import math

import jax
import jax.numpy as jnp
from jax import lax
from jax.sharding import PartitionSpec as P

HEAD = 128
QHEADS = 16
KVHEADS = 4


def attention_block(queries, new_keys, new_values, key_cache, value_cache, cache_lengths, kv_local):
    tokens_here = queries.shape[0]
    cached = key_cache.shape[1]
    group_size = QHEADS // KVHEADS
    query_view = queries.reshape(tokens_here, kv_local, group_size, HEAD)
    all_keys = jnp.concatenate([key_cache[0], new_keys], axis=0).reshape(
        cached + tokens_here, kv_local, HEAD
    )
    all_values = jnp.concatenate([value_cache[0], new_values], axis=0).reshape(
        cached + tokens_here, kv_local, HEAD
    )
    scores = jnp.einsum(
        "tghd,kgd->tghk", query_view, all_keys, preferred_element_type=jnp.float32
    ) / math.sqrt(HEAD)
    position = jnp.arange(cached + tokens_here, dtype=jnp.int32)
    current = jnp.arange(tokens_here, dtype=jnp.int32)
    visible = jnp.where(
        position[None, :] < cached,
        position[None, :] < cache_lengths[0],
        position[None, :] - cached <= current[:, None],
    )
    visible = visible[:, None, None, :]
    highest = jnp.max(jnp.where(visible, scores, -1e30), axis=-1, keepdims=True)
    raised = jnp.exp(jnp.where(visible, scores - highest, -1e30))
    totals = jnp.sum(raised, axis=-1, keepdims=True)
    weights = raised.astype(jnp.bfloat16)
    context = (
        jnp.einsum("tghk,kgd->tghd", weights, all_values, preferred_element_type=jnp.float32)
        / totals
    )
    return context.astype(jnp.bfloat16).reshape(tokens_here, -1)


def normalize(rows_block, norm_gain):
    width_total = rows_block.shape[-1]
    squares = jnp.einsum(
        "secd,secd->sec", rows_block, rows_block, preferred_element_type=jnp.float32
    )
    factor = lax.rsqrt(squares / width_total + 1e-06)
    return (rows_block.astype(jnp.float32) * factor[..., None] * norm_gain).astype(jnp.bfloat16)


def shards(
    queries,
    new_keys,
    new_values,
    key_cache,
    value_cache,
    cache_lengths,
    request_order,
    residual,
    out_weight,
    norm_gain,
    route_experts,
    route_weights,
    expert_gate,
    expert_up,
    expert_down,
):
    tp_count = lax.axis_size("tp")
    ep_count = lax.axis_size("ep")
    kv_local = KVHEADS // tp_count
    context = attention_block(
        queries, new_keys, new_values, key_cache, value_cache, cache_lengths, kv_local
    )
    head_terms = jnp.dot(context, out_weight, preferred_element_type=jnp.float32)
    attended = lax.psum_scatter(head_terms, "tp", scatter_dimension=1, tiled=True)
    hidden_slice = (residual.astype(jnp.float32) + attended).astype(jnp.bfloat16)
    tokens_here, top_count = route_experts.shape
    experts_local = expert_gate.shape[0]
    expert_count = experts_local * ep_count
    capacity = 2 * tokens_here * top_count // expert_count
    flat_routes = route_experts.reshape(-1)
    onehot = (flat_routes[:, None] == jnp.arange(expert_count, dtype=jnp.int32)[None, :]).astype(
        jnp.int32
    )
    ranking = jnp.sum(jnp.cumsum(onehot, axis=0) * onehot, axis=1) - 1
    slot_index = flat_routes * capacity + ranking
    pair_token = jnp.arange(flat_routes.shape[0], dtype=jnp.int32) // top_count
    mixing = (
        (route_weights / jnp.sum(route_weights, axis=1, keepdims=True))
        .astype(jnp.bfloat16)
        .reshape(-1)
    )
    slot_token = jnp.full((expert_count * capacity,), -1, jnp.int32).at[slot_index].set(pair_token)
    slot_mix = jnp.zeros((expert_count * capacity,), jnp.bfloat16).at[slot_index].set(mixing)
    present = slot_token >= 0
    safe_token = jnp.where(present, slot_token, 0)
    inverse = (
        jnp.zeros_like(request_order)
        .at[request_order]
        .set(jnp.arange(request_order.shape[0], dtype=jnp.int32))
    )
    token_range = jnp.arange(tokens_here, dtype=jnp.int32)
    mask_rows = present.astype(jnp.bfloat16)[:, None]
    send_rows = (jnp.take(hidden_slice, safe_token, axis=0) * mask_rows).reshape(
        ep_count, experts_local * capacity, -1
    )
    send_mix = slot_mix.reshape(ep_count, -1)
    send_token = slot_token.reshape(ep_count, -1)
    got_rows, got_mix, got_token = (
        lax.all_to_all(send_rows, "ep", split_axis=0, concat_axis=0, tiled=True),
        lax.all_to_all(send_mix, "ep", split_axis=0, concat_axis=0, tiled=True),
        lax.all_to_all(send_token, "ep", split_axis=0, concat_axis=0, tiled=True),
    )
    full_rows = lax.all_gather(got_rows, "tp", axis=2, tiled=True)
    block_shape = (ep_count, experts_local, capacity)
    normed = normalize(full_rows.reshape(block_shape + (-1,)), norm_gain)
    gate_value = jnp.einsum(
        "secd,edf->secf", normed, expert_gate, preferred_element_type=jnp.float32
    )
    up_value = jnp.einsum("secd,edf->secf", normed, expert_up, preferred_element_type=jnp.float32)
    activation = (jax.nn.silu(gate_value) * up_value).astype(jnp.bfloat16)
    expert_out = jnp.einsum(
        "secf,efd->secd",
        lax.all_gather(activation, "tp", axis=3, tiled=True),
        expert_down,
        preferred_element_type=jnp.float32,
    )
    own_rows = got_rows.reshape(block_shape + (-1,))
    contribution = (
        got_mix.reshape(block_shape).astype(jnp.float32)[..., None]
        * (own_rows.astype(jnp.float32) + expert_out)
    ).astype(jnp.bfloat16)
    back_rows = jnp.take(
        contribution.reshape(ep_count, experts_local * capacity, -1), inverse, axis=0
    )
    back_token = jnp.take(got_token, inverse, axis=0)
    came_rows, came_token = (
        lax.all_to_all(back_rows, "ep", split_axis=0, concat_axis=0, tiled=True),
        lax.all_to_all(back_token, "ep", split_axis=0, concat_axis=0, tiled=True),
    )
    selector = (came_token.reshape(1, -1) == token_range[:, None]).astype(jnp.bfloat16)
    output = jnp.dot(
        selector, came_rows.reshape(selector.shape[1], -1), preferred_element_type=jnp.float32
    ).astype(jnp.bfloat16)
    return output


def solution(mesh):
    return jax.shard_map(
        shards,
        mesh=mesh,
        in_specs=(
            P("ep", "tp"),
            P("ep", "tp"),
            P("ep", "tp"),
            P("ep", None, "tp"),
            P("ep", None, "tp"),
            P("ep"),
            P(),
            P("ep", "tp"),
            P("tp", None),
            P(),
            P("ep", None),
            P("ep", None),
            P("ep", None, "tp"),
            P("ep", None, "tp"),
            P("ep", None, "tp"),
        ),
        out_specs=P("ep", "tp"),
        check_vma=False,
    )
```

profile of v0, /device:TPU:1, one launch (start us, length us, event | category | flops | bytes accessed | tf_op | source)
XLA Modules:
  0.0 271.7 jit_solution(13468024733722653747)
XLA Ops:
  6.5 0.0 copy-start
  6.5 0.0 reduce-scatter.2.cloned.1.call-start
  7.4 0.0 copy-start.3
  7.4 1.3 select_reduce_fusion
  8.7 0.3 fusion.26
  9.0 1.2 fusion.16
  10.3 0.1 copy.45
  10.3 1.3 fusion.43
  11.6 0.0 reduce-scatter.2.cloned.1.call-update
  11.6 0.0 all-gather.3.cloned.1.call-start
  11.7 0.1 copy.35
  11.8 0.1 eq.44
  11.9 0.1 copy.37
  12.0 0.2 fusion.34
  12.3 0.1 eq.40
  12.4 0.1 copy.34
  12.5 0.1 mul.71
  12.6 0.2 fusion.33
  12.8 2.4 scatter_custom_fusion.1
  15.3 0.1 reshape.270
  15.4 0.1 broadcast_in_dim.100
  15.5 26.3 %reduce-scatter.2.cloned.1.call-done = f32[64,512]{1,0:T(8,128)} async-done(((f32[64,2048]{1,0:T(8,128)}), f32[64,512]{1,0:T(8,128)}) %reduce-scatter.2.cloned.1.call-update) | async-done | bytes 131088 | tf_op jit(solution)/shard_map/reduce_scatter | solution.py:79
  41.9 0.9 add_convert_fusion
  42.8 4.0 %gather_fusion.1 = bf16[1024,512]{1,0:T(8,128)(2,1)S(1)} fusion(bf16[64,512]{1,0:T(8,128)(2,1)S(1)} %add_convert_fusion, s32[1024]{0:T(1024)S(1)} %fusion.48), kind=kCustom, calls=%fused_computation.1 | custom fusion | bytes 2101248 | tf_op jit(solution)/shard_map/jit(_take)/gather | solution.py:108
  46.8 0.3 fusion.18
  47.1 0.0 copy-start.6
  47.1 47.0 %all_to_all.38 = bf16[128,8,512]{2,1,0:T(8,128)(2,1)} all-to-all(bf16[128,8,512]{2,1,0:T(8,128)(2,1)S(1)} %fusion.18), channel_id=1, replica_groups=mesh['ep'=128,'tp'=4] {'ep'}, dimensions={0} | all-to-all | bytes 2097152 | tf_op jit(solution)/shard_map/all_to_all | solution.py:114
  94.1 0.0 all-gather.3.cloned.1.call-update
  94.2 0.2 all-gather.5.cloned.1.call-start
  94.4 45.7 %all-gather.3.cloned.1.call-done = bf16[128,8,2048]{2,1,0:T(8,128)(2,1)} async-done(((bf16[128,8,512]{2,1,0:T(8,128)(2,1)}), bf16[128,8,2048]{2,1,0:T(8,128)(2,1)}) %all-gather.3.cloned.1.call-update) | async-done | bytes 4194320 | tf_op jit(solution)/shard_map/all_gather | solution.py:118
  140.1 3.2 %fusion.2 = f32[128,8]{1,0:T(8,128)S(1)} fusion(bf16[128,8,2048]{2,1,0:T(8,128)(2,1)} %all-gather.3.cloned.1.call-done), kind=kLoop, calls=%fused_computation.10 | loop fusion | flops 6290432 | bytes 4198400 | tf_op jit(solution)/shard_map/secd,secd->sec/dot_general | solution.py:48
  143.3 0.2 copy-done.1
  143.5 2.4 fusion.5
  145.9 1.3 copy.55
  147.3 4.7 %fusion.3 = f32[128,8,192]{2,1,0:T(8,128)} fusion(bf16[128,8,2048]{2,1,0:T(8,128)(2,1)} %all-gather.3.cloned.1.call-done, f32[2048]{0:T(1024)S(1)} %copy-done.6, f32[128,8]{1,0:T(8,128)S(1)} %add_rsqrt_fusion, bf16[1,2048,192]{1,2,0:T(8,128)(2,1)} %param.28), kind=kOutput, calls=%fused_computation.11 | convolution fusion | flops 813694976 | bytes 5779456 | tf_op jit(solution)/shard_map/secd,edf->secf/dot_general | solution.py:124
  152.0 2.6 copy.57
  154.5 2.3 fusion.19
  156.9 0.0 all-gather.5.cloned.1.call-update
  156.9 0.1 copy.41
  157.0 0.1 reshape.316
  157.1 3.8 %scatter_custom_fusion.2 = bf16[1024]{0:T(1024)(128)(2,1)S(1)} fusion(s32[512]{0:T(512)S(1)} %bitcast.138, bf16[512]{0:T(512)(128)(2,1)S(1)} %reshape.316, bf16[]{:T(256)} %constant.86.clone.1), kind=kCustom, calls=%fused_computation.98 | custom fusion | bytes 2050 | tf_op jit(solution)/shard_map/scatter | solution.py:98
  160.9 0.7 all_to_all.32
  161.7 14.5 %all-to-all-start.2 = ((bf16[128,1,8]{2,1,0:T(2,128)(2,1)}), bf16[128,1,8]{2,1,0:T(2,128)(2,1)S(1)}, u32[]{:S(2)}, u32[]{:S(2)}) async-start(bf16[128,1,8]{2,1,0:T(2,128)(2,1)} %all_to_all.32), calls=%async_computation.2 | async-start | bytes 131072 | tf_op jit(solution)/shard_map/all_to_all | solution.py:115
  176.2 1.0 scatter_custom_fusion
  177.2 0.7 all_to_all.24
  177.9 9.8 %all-to-all-done.2 = bf16[128,1,8]{2,1,0:T(2,128)(2,1)S(1)} async-done(((bf16[128,1,8]{2,1,0:T(2,128)(2,1)}), bf16[128,1,8]{2,1,0:T(2,128)(2,1)S(1)}, u32[]{:S(2)}, u32[]{:S(2)}) %all-to-all-start.2) | async-done | bytes 2080 | tf_op jit(solution)/shard_map/all_to_all | solution.py:115
  187.6 5.9 %all-to-all-start = ((s32[128,1,8]{2,1,0:T(1,128)}), s32[128,1,8]{2,1,0:T(1,128)S(1)}, u32[]{:S(2)}, u32[]{:S(2)}) async-start(s32[128,1,8]{2,1,0:T(1,128)} %bitcast.5), calls=%async_computation | async-start | bytes 131072 | tf_op jit(solution)/shard_map/all_to_all | solution.py:116
  193.5 0.1 mul.87
  193.7 11.6 %all-to-all-done = s32[128,1,8]{2,1,0:T(1,128)S(1)} async-done(((s32[128,1,8]{2,1,0:T(1,128)}), s32[128,1,8]{2,1,0:T(1,128)S(1)}, u32[]{:S(2)}, u32[]{:S(2)}) %all-to-all-start) | async-done | bytes 4128 | tf_op jit(solution)/shard_map/all_to_all | solution.py:116
  205.2 0.6 gather_fusion
  205.9 0.7 bitcast_select_fusion.2
  206.6 5.7 %all-to-all-start.1 = ((s32[128,1,8]{2,1,0:T(1,128)}), s32[128,1,8]{2,1,0:T(1,128)S(1)}, u32[]{:S(2)}, u32[]{:S(2)}) async-start(s32[128,1,8]{2,1,0:T(1,128)} %bitcast.8), calls=%async_computation.1 | async-start | bytes 131072 | tf_op jit(solution)/shard_map/all_to_all | solution.py:143
  212.3 0.0 all-gather.5.cloned.1.call-done
  212.3 3.0 %fusion.10 = bf16[128,8,512]{2,0,1:T(8,128)(2,1)S(1)} fusion(bf16[128,1,8,768]{0,3,2,1:T(8,128)(2,1)} %all-gather.5.cloned.1.call-done, bf16[128,8,512]{2,1,0:T(8,128)(2,1)S(1)} %copy-done.2, f32[128,8]{0,1:T(8,128)S(1)} %copy.43, bf16[1,768,512]{2,1,0:T(8,128)(2,1)} %param.29), kind=kOutput, calls=%fused_computation.17 | convolution fusion | flops 807403520 | bytes 4460544 | tf_op jit(solution)/shard_map/secf,efd->secd/dot_general | solution.py:126
  215.3 1.6 copy.50
  216.8 1.9 gather_fusion.2
  218.7 1.2 broadcast_select_fusion
  219.9 4.0 %all-to-all-done.1 = s32[128,1,8]{2,1,0:T(1,128)S(1)} async-done(((s32[128,1,8]{2,1,0:T(1,128)}), s32[128,1,8]{2,1,0:T(1,128)S(1)}, u32[]{:S(2)}, u32[]{:S(2)}) %all-to-all-start.1) | async-done | bytes 4128 | tf_op jit(solution)/shard_map/all_to_all | solution.py:143
  223.9 9.9 %all-to-all-start.4 = ((bf16[128,8,512]{2,1,0:T(8,128)(2,1)}), bf16[128,8,512]{2,1,0:T(8,128)(2,1)S(1)}, u32[]{:S(2)}, u32[]{:S(2)}) async-start(bf16[128,8,512]{2,1,0:T(8,128)(2,1)} %broadcast_select_fusion), calls=%async_computation.5 | async-start | bytes 2097152 | tf_op jit(solution)/shard_map/all_to_all | solution.py:142
  233.8 0.5 broadcast.207
  234.3 0.8 reduce.7
  235.1 0.1 eq.48
  235.2 29.0 %all-to-all-done.4 = bf16[128,8,512]{2,1,0:T(8,128)(2,1)S(1)} async-done(((bf16[128,8,512]{2,1,0:T(8,128)(2,1)}), bf16[128,8,512]{2,1,0:T(8,128)(2,1)S(1)}, u32[]{:S(2)}, u32[]{:S(2)}) %all-to-all-start.4) | async-done | bytes 1048608 | tf_op jit(solution)/shard_map/all_to_all | solution.py:142
  264.2 0.9 convolution_convert_fusion
  (36 shorter events, 0.3 us)
Async XLA Ops:
  6.5 3.8 %copy-start = (bf16[512,2048]{1,0:T(8,128)(2,1)S(1)}, bf16[512,2048]{1,0:T(8,128)(2,1)}, u32[]{:S(2)}) copy-start(bf16[512,2048]{1,0:T(8,128)(2,1)} %param.23) | copy-start | bytes 6291460
  6.5 5.1 %copy-start.4 = (s32[64,8]{0,1:T(8,128)S(1)}, s32[64,8]{0,1:T(8,128)}, u32[]{:S(2)}) copy-start(s32[64,8]{0,1:T(8,128)} %param.25) | copy-start | bytes 6148
  6.5 35.3 %reduce-scatter.2.cloned.1.call-start = ((), (), s32[]{:S(2)}) async-start(), calls=%async_computation.6 | async-start | bytes 655360 | tf_op jit(solution)/shard_map/reduce_scatter | solution.py:79
  7.4 34.5 %copy-start.3 = (bf16[64,512]{1,0:T(8,128)(2,1)S(1)}, bf16[64,512]{1,0:T(8,128)(2,1)}, u32[]{:S(2)}) copy-start(bf16[64,512]{1,0:T(8,128)(2,1)} %param.22) | copy-start | bytes 196612
  11.6 128.4 %all-gather.3.cloned.1.call-start = ((), (), s32[]{:S(2)}) async-start(), calls=%async_computation.7 | async-start | bytes 5242880 | tf_op jit(solution)/shard_map/all_gather | solution.py:118
  47.1 96.2 %copy-start.6 = (f32[2048]{0:T(1024)S(1)}, f32[2048]{0:T(1024)}, u32[]{:S(2)}) copy-start(f32[2048]{0:T(1024)} %param.24) | copy-start | bytes 24580
  94.2 118.1 %all-gather.5.cloned.1.call-start = ((), (), s32[]{:S(2)}) async-start(), calls=%async_computation.8 | async-start | bytes 1966080 | tf_op jit(solution)/shard_map/all_gather | solution.py:128
  140.1 3.4 %copy-start.1 = (bf16[128,8,2048]{2,1,0:T(8,128)(2,1)S(1)}, bf16[128,8,2048]{2,1,0:T(8,128)(2,1)}, u32[]{:S(2)}) copy-start(bf16[128,8,2048]{2,1,0:T(8,128)(2,1)} %all-gather.3.cloned.1.call-done) | copy-start | bytes 12582916
  152.0 4.9 %copy-start.5 = (f32[64,8]{0,1:T(8,128)S(1)}, f32[64,8]{0,1:T(8,128)}, u32[]{:S(2)}) copy-start(f32[64,8]{0,1:T(8,128)} %param.26) | copy-start | bytes 6148
  152.0 24.2 %copy-start.7 = (s32[128]{0:T(128)S(1)}, s32[128]{0:T(128)}, u32[]{:S(2)}) copy-start(s32[128]{0:T(128)} %param.21) | copy-start | bytes 1540
  152.0 60.3 %copy-start.2 = (bf16[128,8,512]{2,1,0:T(8,128)(2,1)S(1)}, bf16[128,8,512]{2,1,0:T(8,128)(2,1)}, u32[]{:S(2)}) copy-start(bf16[128,8,512]{2,1,0:T(8,128)(2,1)} %all_to_all.38) | copy-start | bytes 3145732
  161.7 26.0 %all-to-all-start.2 = ((bf16[128,1,8]{2,1,0:T(2,128)(2,1)}), bf16[128,1,8]{2,1,0:T(2,128)(2,1)S(1)}, u32[]{:S(2)}, u32[]{:S(2)}) async-start(bf16[128,1,8]{2,1,0:T(2,128)(2,1)} %all_to_all.32), calls=%async_computation.2 | async-start | bytes 131072 | tf_op jit(solution)/shard_map/all_to_all | solution.py:115
  187.6 17.6 %all-to-all-start = ((s32[128,1,8]{2,1,0:T(1,128)}), s32[128,1,8]{2,1,0:T(1,128)S(1)}, u32[]{:S(2)}, u32[]{:S(2)}) async-start(s32[128,1,8]{2,1,0:T(1,128)} %bitcast.5), calls=%async_computation | async-start | bytes 131072 | tf_op jit(solution)/shard_map/all_to_all | solution.py:116
  206.6 17.3 %all-to-all-start.1 = ((s32[128,1,8]{2,1,0:T(1,128)}), s32[128,1,8]{2,1,0:T(1,128)S(1)}, u32[]{:S(2)}, u32[]{:S(2)}) async-start(s32[128,1,8]{2,1,0:T(1,128)} %bitcast.8), calls=%async_computation.1 | async-start | bytes 131072 | tf_op jit(solution)/shard_map/all_to_all | solution.py:143
  223.9 40.4 %all-to-all-start.4 = ((bf16[128,8,512]{2,1,0:T(8,128)(2,1)}), bf16[128,8,512]{2,1,0:T(8,128)(2,1)S(1)}, u32[]{:S(2)}, u32[]{:S(2)}) async-start(bf16[128,8,512]{2,1,0:T(8,128)(2,1)} %broadcast_select_fusion), calls=%async_computation.5 | async-start | bytes 2097152 | tf_op jit(solution)/shard_map/all_to_all | solution.py:142
Sparse Core Ops, SparseCore 0:
  11.7 30.0 reduce-scatter.1
  94.3 45.7 all-gather.2
  157.0 32.1 all-gather.4
where the time goes:
time: 272 us
  waiting for transfers between devices  126 us (46%)
  blocking collectives  47 us (17%)
  starting transfers between devices  36.2 us (13%)
  local copies, waits for them, and re-layouts  22.5 us (8%)
  matrix products  14.8 us (5%)
  between operations  14.3 us (5%)
  other arithmetic  10.5 us (4%)
    all_to_all x1, blocking collectives, shards(): lax.all_to_all(send_rows, 'ep', split_axis=0, concat_axis=0, tiled=True)  47 us
    all_gather x1, waiting for transfers between devices, shards(): full_rows = lax.all_gather(got_rows, 'tp', axis=2, tiled=True)  45.7 us
    all_to_all x1, waiting for transfers between devices, shards(): lax.all_to_all(back_rows, 'ep', split_axis=0, concat_axis=0, tiled=True)  29 us
    reduce_scatter x1, waiting for transfers between devices, shards(): lax.psum_scatter(head_terms, 'tp', scatter_dimension=1, tiled=True)  26.3 us
    all_to_all x1, starting transfers between devices, shards(): lax.all_to_all(send_mix, 'ep', split_axis=0, concat_axis=0, tiled=True)  14.5 us
    all_to_all x1, waiting for transfers between devices, shards(): lax.all_to_all(send_token, 'ep', split_axis=0, concat_axis=0, tiled=True)  11.6 us
    all_to_all x1, starting transfers between devices, shards(): lax.all_to_all(back_rows, 'ep', split_axis=0, concat_axis=0, tiled=True)  9.88 us
    all_to_all x1, waiting for transfers between devices, shards(): lax.all_to_all(send_mix, 'ep', split_axis=0, concat_axis=0, tiled=True)  9.76 us
  transfers between devices with their start and end apart: 7, of which 6 were waited for; matrix products, arithmetic and copies ran while one was open for 7% of the time, Pallas kernels for 0%

commit v1 on v0

v1 whole, which is shorter than its diff:
```python
import functools
import math

import jax
import jax.numpy as jnp
from jax import lax
from jax.experimental import pallas as pl
from jax.experimental.pallas import tpu as pltpu
from jax.sharding import PartitionSpec as P

HEAD = 128
QHEADS = 16
KVHEADS = 4
CAP = 8
STRIDE = 37
LAG = 4
MESH = pl.DeviceIdType.MESH


def attention_block(queries, new_keys, new_values, key_cache, value_cache, cache_lengths, kv_local):
    tokens_here = queries.shape[0]
    cached = key_cache.shape[1]
    group_size = QHEADS // KVHEADS
    query_view = queries.reshape(tokens_here, kv_local, group_size, HEAD)
    all_keys = jnp.concatenate([key_cache[0], new_keys], axis=0).reshape(
        cached + tokens_here, kv_local, HEAD
    )
    all_values = jnp.concatenate([value_cache[0], new_values], axis=0).reshape(
        cached + tokens_here, kv_local, HEAD
    )
    scores = jnp.einsum(
        "tghd,kgd->tghk", query_view, all_keys, preferred_element_type=jnp.float32
    ) / math.sqrt(HEAD)
    position = jnp.arange(cached + tokens_here, dtype=jnp.int32)
    current = jnp.arange(tokens_here, dtype=jnp.int32)
    visible = jnp.where(
        position[None, :] < cached,
        position[None, :] < cache_lengths[0],
        position[None, :] - cached <= current[:, None],
    )
    visible = visible[:, None, None, :]
    highest = jnp.max(jnp.where(visible, scores, -1e30), axis=-1, keepdims=True)
    raised = jnp.exp(jnp.where(visible, scores - highest, -1e30))
    totals = jnp.sum(raised, axis=-1, keepdims=True)
    weights = raised.astype(jnp.bfloat16)
    context = (
        jnp.einsum("tghk,kgd->tghd", weights, all_values, preferred_element_type=jnp.float32)
        / totals
    )
    return context.astype(jnp.bfloat16).reshape(tokens_here, -1)


def exchange_kernel(tps, x_ref, out_ref, send_sem, recv_sem, own_sem):
    tp = lax.axis_index("tp")
    width = out_ref.shape[2]
    barrier = pltpu.get_barrier_semaphore()
    for o in range(1, tps):
        pl.semaphore_signal(
            barrier, inc=1, device_id={"tp": lax.rem(tp + o, tps)}, device_id_type=MESH
        )
    own = pltpu.make_async_copy(
        x_ref.at[:, pl.ds(pl.multiple_of(tp * width, width), width)], out_ref.at[0], own_sem
    )
    own.start()
    pl.semaphore_wait(barrier, tps - 1)
    copies = []
    for o in range(1, tps):
        peer = lax.rem(tp + o, tps)
        copy = pltpu.make_async_remote_copy(
            src_ref=x_ref.at[:, pl.ds(pl.multiple_of(peer * width, width), width)],
            dst_ref=out_ref.at[o],
            send_sem=send_sem.at[o - 1],
            recv_sem=recv_sem.at[o - 1],
            device_id={"tp": peer},
            device_id_type=MESH,
        )
        copy.start()
        copies.append(copy)
    own.wait()
    for copy in copies:
        copy.wait()


def exchange(terms, tps):
    rows, total = terms.shape
    return pl.pallas_call(
        functools.partial(exchange_kernel, tps),
        out_shape=jax.ShapeDtypeStruct((tps, rows, total // tps), terms.dtype),
        in_specs=[pl.BlockSpec(memory_space=pltpu.VMEM)],
        out_specs=pl.BlockSpec(memory_space=pltpu.VMEM),
        scratch_shapes=[
            pltpu.SemaphoreType.DMA((tps - 1,)),
            pltpu.SemaphoreType.DMA((tps - 1,)),
            pltpu.SemaphoreType.DMA,
        ],
        compiler_params=pltpu.CompilerParams(collective_id=0, has_side_effects=True),
        name="tp_exchange",
    )(terms)


def slot_matrices(experts, mix, count):
    tokens, top = experts.shape
    lanes = lax.broadcasted_iota(jnp.int32, (tokens, count), 1)
    named = jnp.zeros((tokens, count), jnp.float32)
    mixed = jnp.zeros((tokens, count), jnp.float32)
    for k in range(top):
        hit = experts[:, k : k + 1] == lanes
        named = jnp.where(hit, 1.0, named)
        mixed = jnp.where(hit, mix[:, k : k + 1], mixed)
    row = lax.broadcasted_iota(jnp.int32, (tokens, tokens), 0)
    col = lax.broadcasted_iota(jnp.int32, (tokens, tokens), 1)
    earlier = jnp.where(col < row, 1.0, 0.0).astype(jnp.bfloat16)
    rank = jnp.dot(earlier, named.astype(jnp.bfloat16), preferred_element_type=jnp.float32)
    marked = jnp.where(named > 0.0, rank, 255.0).astype(jnp.bfloat16)
    source = lax.broadcasted_iota(jnp.int32, (count, count * CAP), 0)
    target = lax.broadcasted_iota(jnp.int32, (count, count * CAP), 1)
    spread = jnp.where(target // CAP == source, 1.0, 0.0).astype(jnp.bfloat16)
    rank_wide = jnp.dot(marked, spread, preferred_element_type=jnp.float32)
    mix_wide = jnp.dot(mixed.astype(jnp.bfloat16), spread, preferred_element_type=jnp.float32)
    place = lax.rem(
        lax.broadcasted_iota(jnp.int32, (tokens, count * CAP), 1), CAP
    ).astype(jnp.float32)
    chosen = rank_wide == place
    selector = jnp.where(chosen, 1.0, 0.0).astype(jnp.bfloat16)
    weighted = jnp.where(chosen, mix_wide, 0.0).astype(jnp.bfloat16)
    return selector, weighted


def prepare_kernel(count, terms_ref, residual_ref, experts_ref, out_ref):
    total = residual_ref[...].astype(jnp.float32)
    for o in range(terms_ref.shape[0]):
        total = total + terms_ref[o].astype(jnp.float32)
    hidden = total.astype(jnp.bfloat16)
    experts = experts_ref[...]
    selector, _ = slot_matrices(experts, experts.astype(jnp.float32), count)
    rows = lax.dot_general(
        selector, hidden, (((0,), (0,)), ((), ())), preferred_element_type=jnp.float32
    )
    out_ref[...] = rows.reshape(out_ref.shape).astype(jnp.bfloat16)


def prepare(terms, residual, experts, count):
    return pl.pallas_call(
        functools.partial(prepare_kernel, count),
        out_shape=jax.ShapeDtypeStruct((count, CAP, residual.shape[1]), jnp.bfloat16),
        name="prepare",
    )(terms, residual, experts)


def dispatch_kernel(
    eps,
    tps,
    send_ref,
    meta_ref,
    full_ref,
    metas_ref,
    own_sem,
    send_sem,
    meta_send,
    meta_recv,
    recv_sem,
    right_send,
    left_send,
    left_recv,
    right_recv,
    relay_send,
    relay_recv,
):
    ep = lax.axis_index("ep")
    tp = lax.axis_index("tp")
    right = lax.rem(tp + 1, tps)
    left = lax.rem(tp + tps - 1, tps)
    barrier = pltpu.get_barrier_semaphore()

    def greet(k, carry):
        pl.semaphore_signal(
            barrier, inc=1, device_id={"ep": lax.rem(ep + k, eps)}, device_id_type=MESH
        )
        return carry

    for side in (right, left):
        pl.semaphore_signal(barrier, inc=1, device_id={"tp": side}, device_id_type=MESH)
    lax.fori_loop(1, eps, greet, 0)
    own = pltpu.make_async_copy(send_ref.at[ep], full_ref.at[tp, ep], recv_sem.at[0])
    own.start()
    own_meta = pltpu.make_async_copy(meta_ref, metas_ref.at[ep], own_sem)
    own_meta.start()
    pl.semaphore_wait(barrier, eps + 1)

    def offset(k):
        return lax.rem(k * STRIDE, eps)

    def post(k, carry):
        off = offset(k)
        dst = lax.rem(ep + off, eps)
        pltpu.make_async_remote_copy(
            src_ref=send_ref.at[dst],
            dst_ref=full_ref.at[tp, ep],
            send_sem=send_sem,
            recv_sem=recv_sem.at[off],
            device_id={"ep": dst},
            device_id_type=MESH,
        ).start()
        return carry

    def post_meta(k, carry):
        pltpu.make_async_remote_copy(
            src_ref=meta_ref,
            dst_ref=metas_ref.at[ep],
            send_sem=meta_send,
            recv_sem=meta_recv,
            device_id={"ep": lax.rem(ep + offset(k), eps)},
            device_id_type=MESH,
        ).start()
        return carry

    lax.fori_loop(1, eps, post, 0)
    lax.fori_loop(1, eps, post_meta, 0)

    def source(k):
        return lax.rem(ep + eps - offset(k), eps)

    def spread(k):
        src = source(k)
        block = full_ref.at[tp, src]
        pltpu.make_async_copy(block, block, recv_sem.at[offset(k)]).wait()
        for side, ssem, rsem in ((right, right_send, left_recv), (left, left_send, right_recv)):
            pltpu.make_async_remote_copy(
                src_ref=block,
                dst_ref=block,
                send_sem=ssem,
                recv_sem=rsem.at[k],
                device_id={"tp": side},
                device_id_type=MESH,
            ).start()

    def relay(k, way):
        src = source(k)
        from_left = full_ref.at[left, src]
        from_right = full_ref.at[right, src]
        pltpu.make_async_copy(from_left, from_left, left_recv.at[k]).wait()
        pltpu.make_async_copy(from_right, from_right, right_recv.at[k]).wait()
        block, side = ((from_left, right), (from_right, left))[way]
        pltpu.make_async_remote_copy(
            src_ref=block,
            dst_ref=block,
            send_sem=relay_send.at[way],
            recv_sem=relay_recv.at[way],
            device_id={"tp": side},
            device_id_type=MESH,
        ).start()

    for k in range(LAG):
        spread(k)

    def step(i, carry):
        for way in range(2):
            spread(2 * i + way + LAG)
            relay(2 * i + way, way)
        return carry

    lax.fori_loop(0, (eps - LAG) // 2, step, 0)
    for k in range(eps - LAG, eps):
        relay(k, k % 2)

    def drain(ref, sem):
        pltpu.make_async_copy(ref, ref, sem).wait()

    own_meta.wait()
    most = send_ref.at[pl.ds(0, eps - 1)]
    drain(most, send_sem)
    drain(metas_ref.at[pl.ds(0, eps - 1)], meta_send)
    drain(metas_ref.at[pl.ds(0, eps - 1)], meta_recv)
    drain(send_ref, right_send)
    drain(send_ref, left_send)
    half = send_ref.at[pl.ds(0, eps // 2)]
    for way in range(2):
        drain(half, relay_send.at[way])
        drain(half, relay_recv.at[way])


def dispatch(send, meta, eps, tps):
    dma = pltpu.SemaphoreType.DMA
    return pl.pallas_call(
        functools.partial(dispatch_kernel, eps, tps),
        out_shape=(
            jax.ShapeDtypeStruct((tps,) + send.shape, send.dtype),
            jax.ShapeDtypeStruct((eps,) + meta.shape, meta.dtype),
        ),
        in_specs=[pl.BlockSpec(memory_space=pl.ANY)] * 2,
        out_specs=(pl.BlockSpec(memory_space=pl.ANY),) * 2,
        scratch_shapes=[
            dma, dma, dma, dma, dma((eps,)), dma, dma, dma((eps,)), dma((eps,)), dma((2,)), dma((2,))
        ],
        compiler_params=pltpu.CompilerParams(collective_id=1, has_side_effects=True),
        name="dispatch",
    )(send, meta)


def expert_in_kernel(rows_ref, gain_ref, gate_ref, up_ref, out_ref):
    parts, sources, cap, width = rows_ref.shape
    rows = sources * cap
    total = parts * width
    wide = [rows_ref[p].astype(jnp.float32).reshape(rows, width) for p in range(parts)]
    squares = sum(jnp.sum(part * part, axis=1, keepdims=True) for part in wide)
    factor = lax.rsqrt(squares / total + 1e-06)
    normed = jnp.concatenate(
        [
            (part * factor * gain_ref[:, p * width : (p + 1) * width]).astype(jnp.bfloat16)
            for p, part in enumerate(wide)
        ],
        axis=1,
    )
    dims = (((0,), (1,)), ((), ()))
    gate = lax.dot_general(gate_ref[...], normed, dims, preferred_element_type=jnp.float32)
    up = lax.dot_general(up_ref[...], normed, dims, preferred_element_type=jnp.float32)
    out_ref[...] = (gate / (1.0 + jnp.exp(-gate)) * up).astype(jnp.bfloat16)


def expert_in(full, gain, gate, up):
    parts, sources, cap, width = full.shape
    tiles = 4 if sources >= 64 else 1
    part_rows = sources // tiles
    ff = gate.shape[1]
    return pl.pallas_call(
        expert_in_kernel,
        grid=(tiles,),
        out_shape=jax.ShapeDtypeStruct((ff, sources * cap), jnp.bfloat16),
        in_specs=[
            pl.BlockSpec((parts, part_rows, cap, width), lambda i: (0, i, 0, 0)),
            pl.BlockSpec((1, gain.shape[1]), lambda i: (0, 0)),
            pl.BlockSpec(gate.shape, lambda i: (0, 0)),
            pl.BlockSpec(up.shape, lambda i: (0, 0)),
        ],
        out_specs=pl.BlockSpec((ff, part_rows * cap), lambda i: (0, i)),
        name="expert_in",
    )(full, gain, gate, up)


def gather_kernel(tps, chunks, x_ref, out_ref, own_sem, send_sem, recv_sem, relay_send, relay_recv):
    tp = lax.axis_index("tp")
    right = lax.rem(tp + 1, tps)
    left = lax.rem(tp + tps - 1, tps)
    sides = (right, left)
    barrier = pltpu.get_barrier_semaphore()
    for side in sides:
        pl.semaphore_signal(barrier, inc=1, device_id={"tp": side}, device_id_type=MESH)
    own = pltpu.make_async_copy(x_ref, out_ref.at[tp], own_sem)
    own.start()
    pl.semaphore_wait(barrier, 2)
    size = x_ref.shape[0] // chunks
    copies = []
    for c in range(chunks):
        part = pl.ds(c * size, size)
        pair = []
        for way in range(2):
            copy = pltpu.make_async_remote_copy(
                src_ref=x_ref.at[part],
                dst_ref=out_ref.at[tp, part],
                send_sem=send_sem.at[way, c],
                recv_sem=recv_sem.at[way, c],
                device_id={"tp": sides[way]},
                device_id_type=MESH,
            )
            copy.start()
            pair.append(copy)
        copies.append(pair)
    relays = []
    for c in range(chunks):
        part = pl.ds(c * size, size)
        way = c % 2
        for pair in copies[c]:
            pair.wait_recv()
        block = out_ref.at[(left, right)[way], part]
        copy = pltpu.make_async_remote_copy(
            src_ref=block,
            dst_ref=block,
            send_sem=relay_send.at[c],
            recv_sem=relay_recv.at[c],
            device_id={"tp": sides[way]},
            device_id_type=MESH,
        )
        copy.start()
        relays.append(copy)
    own.wait()
    for pair in copies:
        for copy in pair:
            copy.wait_send()
    for copy in relays:
        copy.wait()


def gather(x, tps):
    chunks = 4 if x.shape[0] % 64 == 0 else 2
    dma = pltpu.SemaphoreType.DMA
    return pl.pallas_call(
        functools.partial(gather_kernel, tps, chunks),
        out_shape=jax.ShapeDtypeStruct((tps,) + x.shape, x.dtype),
        in_specs=[pl.BlockSpec(memory_space=pltpu.VMEM)],
        out_specs=pl.BlockSpec(memory_space=pltpu.VMEM),
        scratch_shapes=[dma, dma((2, chunks)), dma((2, chunks)), dma((chunks,)), dma((chunks,))],
        compiler_params=pltpu.CompilerParams(collective_id=2, has_side_effects=True),
        name="tp_gather",
    )(x)


def expert_out_kernel(order_ref, act_ref, down_ref, own_ref, out_ref):
    sources, cap, width = own_ref.shape
    base = pl.program_id(0) * sources
    value = lax.dot_general(
        act_ref[...], down_ref[...], (((0,), (0,)), ((), ())), preferred_element_type=jnp.float32
    )
    value = value.reshape(sources, cap, width) + own_ref[...].astype(jnp.float32)
    value = value.astype(jnp.bfloat16)
    for j in range(sources):
        out_ref[order_ref[base + j]] = value[j]


def expert_out(order, act, down, full, tp):
    parts, sources, cap, width = full.shape
    tiles = 4 if sources >= 64 else 1
    part_rows = sources // tiles
    return pl.pallas_call(
        lambda order_ref, tp_ref, act_ref, down_ref, own_ref, out_ref: expert_out_kernel(
            order_ref, act_ref, down_ref, own_ref, out_ref
        ),
        grid_spec=pltpu.PrefetchScalarGridSpec(
            num_scalar_prefetch=2,
            grid=(tiles,),
            in_specs=[
                pl.BlockSpec((act.shape[0], part_rows * cap), lambda i, o, t: (0, i)),
                pl.BlockSpec(down.shape, lambda i, o, t: (0, 0)),
                pl.BlockSpec((None, part_rows, cap, width), lambda i, o, t: (t[0], i, 0, 0)),
            ],
            out_specs=pl.BlockSpec((sources, cap, width), lambda i, o, t: (0, 0, 0)),
        ),
        out_shape=jax.ShapeDtypeStruct((sources, cap, width), jnp.bfloat16),
        name="expert_out",
    )(order, tp, act, down, full)


def give_back_kernel(eps, send_ref, came_ref, own_sem, send_sem, recv_sem):
    ep = lax.axis_index("ep")
    barrier = pltpu.get_barrier_semaphore()

    def greet(k, carry):
        pl.semaphore_signal(
            barrier, inc=1, device_id={"ep": lax.rem(ep + k, eps)}, device_id_type=MESH
        )
        return carry

    lax.fori_loop(1, eps, greet, 0)
    own = pltpu.make_async_copy(send_ref.at[ep], came_ref.at[ep], own_sem)
    own.start()
    pl.semaphore_wait(barrier, eps - 1)

    def post(k, carry):
        dst = lax.rem(ep + lax.rem(k * STRIDE, eps), eps)
        pltpu.make_async_remote_copy(
            src_ref=send_ref.at[dst],
            dst_ref=came_ref.at[ep],
            send_sem=send_sem,
            recv_sem=recv_sem,
            device_id={"ep": dst},
            device_id_type=MESH,
        ).start()
        return carry

    lax.fori_loop(1, eps, post, 0)
    own.wait()
    most = send_ref.at[pl.ds(0, eps - 1)]
    pltpu.make_async_copy(most, most, send_sem).wait()
    pltpu.make_async_copy(most, most, recv_sem).wait()


def give_back(send, eps):
    dma = pltpu.SemaphoreType.DMA
    return pl.pallas_call(
        functools.partial(give_back_kernel, eps),
        out_shape=jax.ShapeDtypeStruct(send.shape, send.dtype),
        in_specs=[pl.BlockSpec(memory_space=pl.ANY)],
        out_specs=pl.BlockSpec(memory_space=pl.ANY),
        scratch_shapes=[dma, dma, dma],
        compiler_params=pltpu.CompilerParams(collective_id=3, has_side_effects=True),
        name="give_back",
    )(send)


def combine_kernel(experts_ref, mix_ref, came_ref, out_ref):
    count, cap, width = came_ref.shape
    _, weighted = slot_matrices(experts_ref[...], mix_ref[...], count)
    rows = came_ref[...].astype(jnp.float32).reshape(count * cap, width).astype(jnp.bfloat16)
    out_ref[...] = jnp.dot(weighted, rows, preferred_element_type=jnp.float32).astype(jnp.bfloat16)


def combine(experts, mix, came):
    return pl.pallas_call(
        combine_kernel,
        out_shape=jax.ShapeDtypeStruct((experts.shape[0], came.shape[2]), jnp.bfloat16),
        name="combine",
    )(experts, mix, came)


def shards(
    queries,
    new_keys,
    new_values,
    key_cache,
    value_cache,
    cache_lengths,
    request_order,
    residual,
    out_weight,
    norm_gain,
    route_experts,
    route_weights,
    expert_gate,
    expert_up,
    expert_down,
):
    tps = lax.axis_size("tp")
    eps = lax.axis_size("ep")
    ep = lax.axis_index("ep")
    tp = lax.axis_index("tp")
    context = attention_block(
        queries, new_keys, new_values, key_cache, value_cache, cache_lengths, KVHEADS // tps
    )
    head_terms = jnp.dot(context, out_weight, preferred_element_type=jnp.float32)
    terms = exchange(head_terms.astype(jnp.bfloat16), tps)
    tokens, top = route_experts.shape
    mixing = (route_weights / jnp.sum(route_weights, axis=1, keepdims=True)).astype(jnp.bfloat16)
    meta = jnp.concatenate(
        [route_experts.astype(jnp.bfloat16).reshape(-1), mixing.reshape(-1)]
    )
    pairs = tokens * top
    meta = jnp.pad(meta, (0, -(2 * pairs) % 1024)).reshape(-1, 128)
    send = prepare(terms, residual, route_experts, eps)
    full, metas = dispatch(send, meta, eps, tps)
    act = expert_in(full, norm_gain[None, :], expert_gate[0], expert_up[0])
    act_full = gather(act, tps).reshape(-1, act.shape[1])
    back = expert_out(request_order, act_full, expert_down[0], full, tp[None].astype(jnp.int32))
    came = give_back(back, eps)
    origin = jnp.argmax(request_order == ep).astype(jnp.int32)
    theirs = lax.dynamic_index_in_dim(metas, origin, 0, keepdims=False).reshape(-1)
    their_experts = theirs[:pairs].reshape(tokens, top).astype(jnp.int32)
    their_mix = theirs[pairs : 2 * pairs].reshape(tokens, top).astype(jnp.float32)
    return combine(their_experts, their_mix, came)


def solution(mesh):
    return jax.shard_map(
        shards,
        mesh=mesh,
        in_specs=(
            P("ep", "tp"),
            P("ep", "tp"),
            P("ep", "tp"),
            P("ep", None, "tp"),
            P("ep", None, "tp"),
            P("ep"),
            P(),
            P("ep", "tp"),
            P("tp", None),
            P(),
            P("ep", None),
            P("ep", None),
            P("ep", None, "tp"),
            P("ep", None, "tp"),
            P("ep", None, "tp"),
        ),
        out_specs=P("ep", "tp"),
        check_vma=False,
    )
```

time: 272 us -> 221 us (0.81)
  Pallas kernels: 0 us -> 206 us
  waiting for transfers between devices: 126 us -> 0 us
  blocking collectives: 47 us -> 0 us
  starting transfers between devices: 36.2 us -> 0 us
  local copies, waits for them, and re-layouts: 22.5 us -> 6.79 us
  between operations: 14.3 us -> 2.79 us
  matrix products: 14.8 us -> 3.71 us
  other arithmetic: 10.5 us -> 1.61 us
    pallas_call x0 -> x8, Pallas kernels: none -> 206 us  [the longest x1 107 us: dispatch(): pl.pallas_call(functools.partial(dispatch_kernel, eps, tps), out_shape=(j...]
    all_to_all x4 -> x0, waiting for transfers between devices: 54.3 us -> none  [the longest x1 29 us: shards(): lax.all_to_all(back_rows, 'ep', split_axis=0, concat_axis=0, tiled=True)]
    all_to_all x1 -> x0, blocking collectives: 47 us -> none  [shards(): lax.all_to_all(send_rows, 'ep', split_axis=0, concat_axis=0, tiled=True)]
    all_gather x2 -> x0, waiting for transfers between devices: 45.7 us -> none  [the longest x1 45.7 us: shards(): full_rows = lax.all_gather(got_rows, 'tp', axis=2, tiled=True)]
    all_to_all x4 -> x0, starting transfers between devices: 35.9 us -> none  [the longest x1 14.5 us: shards(): lax.all_to_all(send_mix, 'ep', split_axis=0, concat_axis=0, tiled=True)]
    reduce_scatter x1 -> x0, waiting for transfers between devices: 26.3 us -> none  [shards(): lax.psum_scatter(head_terms, 'tp', scatter_dimension=1, tiled=True)]
    dot_general x4 -> x0, matrix products: 11 us -> none  [the longest x1 4.71 us: shards(): jnp.einsum('secd,edf->secf', normed, expert_up, preferred_element_type=jn...]
    scatter x3 -> x0, local copies, waits for them, and re-layouts: 7.19 us -> none  [the longest x1 3.77 us: shards(): jnp.zeros((expert_count * capacity,), jnp.bfloat16).at[slot_index]]
  transfers between devices with their start and end apart: 7 -> 0, of which waited for: 6 -> 0; matrix products, arithmetic and copies ran while one was open for 7% -> 0% of each run, Pallas kernels for 0% -> 0%
where the time goes in v1:
time: 221 us
  Pallas kernels  206 us (93%)
  local copies, waits for them, and re-layouts  6.79 us (3%)
  matrix products  3.71 us (2%)
  between operations  2.79 us (1%)
    pallas_call x1, Pallas kernels, dispatch(): pl.pallas_call(functools.partial(dispatch_kernel, eps, tps), out_shape=(j...  107 us
    pallas_call x1, Pallas kernels, give_back(): pl.pallas_call(functools.partial(give_back_kernel, eps), out_shape=jax.Sh...  57.9 us
    pallas_call x1, Pallas kernels, gather(): pl.pallas_call(functools.partial(gather_kernel, tps, chunks), out_shape=j...  13.6 us
    pallas_call x1, Pallas kernels, exchange(): pl.pallas_call(functools.partial(exchange_kernel, tps), out_shape=jax.Sha...  9.36 us
    pallas_call x1, Pallas kernels, expert_in(): pl.pallas_call(expert_in_kernel, grid=(tiles,), out_shape=jax.ShapeDtypeS...  7.12 us
    pallas_call x1, Pallas kernels, expert_out(): pl.pallas_call(lambda order_ref, tp_ref, act_ref, down_ref, own_ref, out_...  5.38 us

profile of v1, /device:TPU:1, one launch (start us, length us, event | category | flops | bytes accessed | tf_op | source)
XLA Modules:
  0.0 220.6 jit_solution(17647429857575453332)
XLA Ops:
  0.0 0.0 copy-start
  0.9 1.3 select_reduce_fusion
  2.1 0.3 fusion.4
  2.4 0.0 copy-start.2
  2.4 1.3 fusion.3
  3.7 0.1 copy.23
  3.8 0.0 copy-done
  3.8 0.0 copy-start.3
  3.8 1.2 convolution_convert_fusion.x_ref
  5.0 0.0 copy-start.4
  5.0 0.0 copy-start.1
  5.0 9.4 %tp_exchange.1.terms_ref = bf16[4,64,512]{2,1,0:T(8,128)(2,1)} custom-call(bf16[64,2048]{1,0:T(8,128)(2,1)} %convolution_convert_fusion.x_ref), custom_call_target="tpu_custom_call" | custom-call | tf_op jit(solution)/shard_map/tp_exchange/pallas_call | solution.py:86
  14.3 0.0 copy-done.2
  14.3 0.7 copy.24.experts_ref
  15.0 2.9 %prepare.1.send_ref = bf16[128,8,512]{2,1,0:T(8,128)(2,1)} custom-call(bf16[4,64,512]{2,1,0:T(8,128)(2,1)} %tp_exchange.1.terms_ref, bf16[64,512]{1,0:T(8,128)(2,1)} %residual_ref.1, s32[64,8]{1,0:T(8,128)} %copy.24.experts_ref), custom_call_target="tpu_custom_call" | custom-call | tf_op jit(solution)/shard_map/prepare/pallas_call | solution.py:143
  17.9 0.0 copy-done.3
  17.9 0.1 copy.26
  18.0 0.1 concatenate.17
  18.1 0.1 copy.25
  18.2 0.1 concatenate.16
  18.3 0.6 pad_maximum_fusion.meta_ref
  18.9 106.9 %dispatch.1 = (bf16[4,128,8,512]{3,2,1,0:T(8,128)(2,1)}, bf16[128,8,128]{2,1,0:T(8,128)(2,1)}) custom-call(bf16[128,8,512]{2,1,0:T(8,128)(2,1)} %prepare.1.send_ref, bf16[8,128]{1,0:T(8,128)(2,1)} %pad_maximum_fusion.meta_ref), custom_call_target="tpu_custom_call" | custom-call | tf_op jit(solution)/shard_map/dispatch/pallas_call | solution.py:284
  125.8 0.0 copy-done.4
  125.9 0.7 compare_reduce_fusion
  128.4 0.7 constant_dynamic-slice_fusion
  129.1 0.7 reshape.115.experts_ref
  129.7 0.7 reshape.116.mix_ref
  130.4 0.0 copy-done.1
  130.4 1.3 copy.27
  131.8 2.2 %copy.28 = bf16[1,2048,192]{2,1,0:T(8,128)(2,1)} copy(bf16[1,2048,192]{1,2,0:T(8,128)(2,1)} %param.28) | data formatting | bytes 1572864 | tf_op args[13]
  134.0 7.1 %expert_in.1.x_ref = bf16[192,1024]{1,0:T(8,128)(2,1)} custom-call(bf16[4,128,8,512]{3,2,1,0:T(8,128)(2,1)} %get-tuple-element.10.rows_ref.own_ref, f32[1,2048]{1,0:T(1,128)} %bitcast.56, bf16[2048,192]{1,0:T(8,128)(2,1)} %bitcast.52, bf16[2048,192]{1,0:T(8,128)(2,1)} %bitcast.53), custom_call_target="tpu_custom_call" | custom-call | tf_op jit(solution)/shard_map/expert_in/pallas_call | solution.py:325
  141.1 13.6 %tp_gather.1 = bf16[4,192,1024]{2,1,0:T(8,128)(2,1)} custom-call(bf16[192,1024]{1,0:T(8,128)(2,1)} %expert_in.1.x_ref), custom_call_target="tpu_custom_call" | custom-call | tf_op jit(solution)/shard_map/tp_gather/pallas_call | solution.py:396
  154.7 5.4 %expert_out.1.send_ref = bf16[128,8,512]{2,1,0:T(8,128)(2,1)} custom-call(s32[128]{0:T(128)} %order_ref.1, s32[1]{0:T(128)} %bitcast.11.tp_ref, bf16[768,1024]{1,0:T(8,128)(2,1)} %bitcast.51, bf16[768,512]{1,0:T(8,128)(2,1)} %bitcast.54, bf16[4,128,8,512]{3,2,1,0:T(8,128)(2,1)} %get-tuple-element.10.rows_ref.own_ref), custom_call_target="tpu_custom_call" | custom-call | tf_op jit(solution)/shard_map/expert_out/pallas_call | solution.py:423
  160.1 57.9 %give_back.1.came_ref = bf16[128,8,512]{2,1,0:T(8,128)(2,1)} custom-call(bf16[128,8,512]{2,1,0:T(8,128)(2,1)} %expert_out.1.send_ref), custom_call_target="tpu_custom_call" | custom-call | tf_op jit(solution)/shard_map/give_back/pallas_call | solution.py:478
  218.0 2.6 %combine.1 = bf16[64,512]{1,0:T(8,128)(2,1)} custom-call(s32[64,8]{1,0:T(8,128)} %reshape.115.experts_ref, f32[64,8]{1,0:T(8,128)} %reshape.116.mix_ref, bf16[128,8,512]{2,1,0:T(8,128)(2,1)} %give_back.1.came_ref), custom_call_target="tpu_custom_call" | custom-call | tf_op jit(solution)/shard_map/combine/pallas_call | solution.py:497
  (7 shorter events, 0.1 us)
Async XLA Ops:
  0.0 3.8 %copy-start = (bf16[512,2048]{1,0:T(8,128)(2,1)S(1)}, bf16[512,2048]{1,0:T(8,128)(2,1)}, u32[]{:S(2)}) copy-start(bf16[512,2048]{1,0:T(8,128)(2,1)} %param.23) | copy-start | bytes 6291460
  2.4 11.9 %copy-start.2 = (s32[64,8]{0,1:T(8,128)S(1)}, s32[64,8]{0,1:T(8,128)}, u32[]{:S(2)}) copy-start(s32[64,8]{0,1:T(8,128)} %param.25) | copy-start | bytes 6148
  3.8 14.1 %copy-start.3 = (f32[64,8]{0,1:T(8,128)S(1)}, f32[64,8]{0,1:T(8,128)}, u32[]{:S(2)}) copy-start(f32[64,8]{0,1:T(8,128)} %param.26) | copy-start | bytes 6148
  5.0 120.9 %copy-start.4 = (s32[128]{0:T(128)S(1)}, s32[128]{0:T(128)}, u32[]{:S(2)}) copy-start(s32[128]{0:T(128)} %order_ref.1) | copy-start | bytes 1540
  5.0 125.5 %copy-start.1 = (bf16[1,2048,192]{1,2,0:T(8,128)(2,1)S(1)}, bf16[1,2048,192]{1,2,0:T(8,128)(2,1)}, u32[]{:S(2)}) copy-start(bf16[1,2048,192]{1,2,0:T(8,128)(2,1)} %param.27) | copy-start | bytes 2359300

commit v2 on v1

--- a/solution.py
+++ b/solution.py
@@ -13,7 +13,8 @@
 KVHEADS = 4
 CAP = 8
 STRIDE = 37
-LAG = 4
+LAG = 32
+AHEAD = 48
 MESH = pl.DeviceIdType.MESH
 
 
@@ -48,6 +49,10 @@
         / totals
     )
     return context.astype(jnp.bfloat16).reshape(tokens_here, -1)
+
+
+def row_span(eps):
+    return 16 if eps > 16 else 2
 
 
 def exchange_kernel(tps, x_ref, out_ref, send_sem, recv_sem, own_sem):
@@ -185,12 +190,19 @@
     own.start()
     own_meta = pltpu.make_async_copy(meta_ref, metas_ref.at[ep], own_sem)
     own_meta.start()
+    span = row_span(eps)
+    rows = eps // span
+    row = lax.div(ep, span)
+    place = lax.rem(ep, span)
     pl.semaphore_wait(barrier, eps + 1)
 
     def offset(k):
         return lax.rem(k * STRIDE, eps)
 
-    def post(k, carry):
+    def source(k):
+        return lax.rem(ep + eps - offset(k), eps)
+
+    def post(k):
         off = offset(k)
         dst = lax.rem(ep + off, eps)
         pltpu.make_async_remote_copy(
@@ -201,28 +213,32 @@
             device_id={"ep": dst},
             device_id_type=MESH,
         ).start()
-        return carry
-
-    def post_meta(k, carry):
+
+    def meta_near(k, carry):
         pltpu.make_async_remote_copy(
             src_ref=meta_ref,
             dst_ref=metas_ref.at[ep],
-            send_sem=meta_send,
-            recv_sem=meta_recv,
-            device_id={"ep": lax.rem(ep + offset(k), eps)},
+            send_sem=meta_send.at[0],
+            recv_sem=meta_recv.at[0],
+            device_id={"ep": row * span + lax.rem(place + k, span)},
             device_id_type=MESH,
         ).start()
         return carry
 
-    lax.fori_loop(1, eps, post, 0)
-    lax.fori_loop(1, eps, post_meta, 0)
-
-    def source(k):
-        return lax.rem(ep + eps - offset(k), eps)
+    def meta_far(k, carry):
+        ours = metas_ref.at[pl.ds(row * span, span)]
+        pltpu.make_async_remote_copy(
+            src_ref=ours,
+            dst_ref=ours,
+            send_sem=meta_send.at[1],
+            recv_sem=meta_recv.at[1],
+            device_id={"ep": lax.rem(row + k, rows) * span + place},
+            device_id_type=MESH,
+        ).start()
+        return carry
 
     def spread(k):
-        src = source(k)
-        block = full_ref.at[tp, src]
+        block = full_ref.at[tp, source(k)]
         pltpu.make_async_copy(block, block, recv_sem.at[offset(k)]).wait()
         for side, ssem, rsem in ((right, right_send, left_recv), (left, left_send, right_recv)):
             pltpu.make_async_remote_copy(
@@ -250,27 +266,50 @@
             device_id_type=MESH,
         ).start()
 
-    for k in range(LAG):
-        spread(k)
-
-    def step(i, carry):
-        for way in range(2):
-            spread(2 * i + way + LAG)
-            relay(2 * i + way, way)
-        return carry
-
-    lax.fori_loop(0, (eps - LAG) // 2, step, 0)
-    for k in range(eps - LAG, eps):
-        relay(k, k % 2)
-
     def drain(ref, sem):
         pltpu.make_async_copy(ref, ref, sem).wait()
 
+    def pairs(low, high, step):
+        def both(i, carry):
+            for way in range(2):
+                step(2 * i + way, way)
+            return carry
+
+        lax.fori_loop(low // 2, high // 2, both, 0)
+
+    def first(k, carry):
+        post(k)
+        return carry
+
+    def opening(k, way):
+        post(k + ahead)
+        spread(k)
+
+    def middle(k, way):
+        post(k + ahead)
+        spread(k)
+        relay(k - lag, way)
+
+    def closing(k, way):
+        spread(k)
+        relay(k - lag, way)
+
+    ahead, lag = min(AHEAD, eps // 2), min(LAG, eps // 2)
+    lax.fori_loop(1, ahead, first, 0)
+    lax.fori_loop(1, span, meta_near, 0)
+    pairs(0, lag, opening)
+    pairs(lag, eps - ahead, middle)
     own_meta.wait()
-    most = send_ref.at[pl.ds(0, eps - 1)]
-    drain(most, send_sem)
-    drain(metas_ref.at[pl.ds(0, eps - 1)], meta_send)
-    drain(metas_ref.at[pl.ds(0, eps - 1)], meta_recv)
+    near = metas_ref.at[pl.ds(0, span - 1)]
+    drain(near, meta_recv.at[0])
+    lax.fori_loop(1, rows, meta_far, 0)
+    pairs(eps - ahead, eps, closing)
+    pairs(eps - lag, eps, relay)
+    drain(near, meta_send.at[0])
+    far = metas_ref.at[pl.ds(0, (rows - 1) * span)]
+    drain(far, meta_send.at[1])
+    drain(far, meta_recv.at[1])
+    drain(send_ref.at[pl.ds(0, eps - 1)], send_sem)
     drain(send_ref, right_send)
     drain(send_ref, left_send)
     half = send_ref.at[pl.ds(0, eps // 2)]
@@ -290,7 +329,7 @@
         in_specs=[pl.BlockSpec(memory_space=pl.ANY)] * 2,
         out_specs=(pl.BlockSpec(memory_space=pl.ANY),) * 2,
         scratch_shapes=[
-            dma, dma, dma, dma, dma((eps,)), dma, dma, dma((eps,)), dma((eps,)), dma((2,)), dma((2,))
+            dma, dma, dma((2,)), dma((2,)), dma((eps,)), dma, dma, dma((eps,)), dma((eps,)), dma((2,)), dma((2,))
         ],
         compiler_params=pltpu.CompilerParams(collective_id=1, has_side_effects=True),
         name="dispatch",
@@ -311,7 +350,7 @@
         ],
         axis=1,
     )
-    dims = (((0,), (1,)), ((), ()))
+    dims = (((1,), (1,)), ((), ()))
     gate = lax.dot_general(gate_ref[...], normed, dims, preferred_element_type=jnp.float32)
     up = lax.dot_general(up_ref[...], normed, dims, preferred_element_type=jnp.float32)
     out_ref[...] = (gate / (1.0 + jnp.exp(-gate)) * up).astype(jnp.bfloat16)
@@ -321,7 +360,7 @@
     parts, sources, cap, width = full.shape
     tiles = 4 if sources >= 64 else 1
     part_rows = sources // tiles
-    ff = gate.shape[1]
+    ff = gate.shape[0]
     return pl.pallas_call(
         expert_in_kernel,
         grid=(tiles,),
@@ -536,7 +575,7 @@
     meta = jnp.pad(meta, (0, -(2 * pairs) % 1024)).reshape(-1, 128)
     send = prepare(terms, residual, route_experts, eps)
     full, metas = dispatch(send, meta, eps, tps)
-    act = expert_in(full, norm_gain[None, :], expert_gate[0], expert_up[0])
+    act = expert_in(full, norm_gain[None, :], expert_gate[0].T, expert_up[0].T)
     act_full = gather(act, tps).reshape(-1, act.shape[1])
     back = expert_out(request_order, act_full, expert_down[0], full, tp[None].astype(jnp.int32))
     came = give_back(back, eps)

time: 221 us -> 163 us (0.74)
  Pallas kernels: 206 us -> 147 us
  local copies, waits for them, and re-layouts: 6.79 us -> 3.91 us
  other arithmetic: 1.61 us -> 4.41 us
    pallas_call x1, Pallas kernels: 107 us -> 61.9 us  [dispatch(): pl.pallas_call(functools.partial(dispatch_kernel, eps, tps), out_shape=(j...]
    pallas_call x1, Pallas kernels: 57.9 us -> 43.7 us  [give_back(): pl.pallas_call(functools.partial(give_back_kernel, eps), out_shape=jax.Sh...]
    unnamed x13 -> x3, local copies, waits for them, and re-layouts: 4.26 us -> 1.39 us
where the time goes in v2:
time: 163 us; the launch traced here: 162 us
  Pallas kernels  147 us (90%)
  other arithmetic  4.41 us (3%)
  local copies, waits for them, and re-layouts  3.91 us (2%)
  matrix products  3.71 us (2%)
  between operations  2.56 us (2%)
    pallas_call x1, Pallas kernels, dispatch(): pl.pallas_call(functools.partial(dispatch_kernel, eps, tps), out_shape=(j...  61.9 us
    pallas_call x1, Pallas kernels, give_back(): pl.pallas_call(functools.partial(give_back_kernel, eps), out_shape=jax.Sh...  43.7 us
    pallas_call x1, Pallas kernels, gather(): pl.pallas_call(functools.partial(gather_kernel, tps, chunks), out_shape=j...  14.6 us
    pallas_call x1, Pallas kernels, exchange(): pl.pallas_call(functools.partial(exchange_kernel, tps), out_shape=jax.Sha...  9.22 us
    pallas_call x1, Pallas kernels, expert_in(): pl.pallas_call(expert_in_kernel, grid=(tiles,), out_shape=jax.ShapeDtypeS...  7 us
    pallas_call x1, Pallas kernels, expert_out(): pl.pallas_call(lambda order_ref, tp_ref, act_ref, down_ref, own_ref, out_...  5.38 us

profile of v2, /device:TPU:1, one launch (start us, length us, event | category | flops | bytes accessed | tf_op | source)
XLA Modules:
  0.0 161.9 jit_solution(4226634305299638445)
XLA Ops:
  0.0 0.0 copy-start
  0.8 0.7 reduce_sum.19
  1.5 1.4 compare_reduce_fusion
  4.6 0.7 divide_convert_fusion
  5.3 0.7 convert_element_type.32
  6.0 0.1 copy.23
  6.1 0.1 concatenate.16
  6.2 0.1 copy.24
  6.3 0.1 concatenate.17
  6.4 0.6 pad_maximum_fusion.meta_ref
  7.0 1.4 copy.22.experts_ref
  8.4 1.3 select_reduce_fusion
  9.7 0.3 fusion.4
  10.0 1.2 fusion.3
  11.2 0.1 copy.21
  11.3 0.0 copy-done
  11.3 1.2 convolution_convert_fusion.x_ref
  12.5 9.2 %tp_exchange.1.terms_ref = bf16[4,64,512]{2,1,0:T(8,128)(2,1)} custom-call(bf16[64,2048]{1,0:T(8,128)(2,1)} %convolution_convert_fusion.x_ref), custom_call_target="tpu_custom_call" | custom-call | tf_op jit(solution)/shard_map/tp_exchange/pallas_call | solution.py:91
  21.7 2.9 %prepare.1.send_ref = bf16[128,8,512]{2,1,0:T(8,128)(2,1)} custom-call(bf16[4,64,512]{2,1,0:T(8,128)(2,1)} %tp_exchange.1.terms_ref, bf16[64,512]{1,0:T(8,128)(2,1)} %residual_ref.1, s32[64,8]{1,0:T(8,128)} %copy.22.experts_ref), custom_call_target="tpu_custom_call" | custom-call | tf_op jit(solution)/shard_map/prepare/pallas_call | solution.py:148
  24.6 61.9 %dispatch.1 = (bf16[4,128,8,512]{3,2,1,0:T(8,128)(2,1)}, bf16[128,8,128]{2,1,0:T(8,128)(2,1)}) custom-call(bf16[128,8,512]{2,1,0:T(8,128)(2,1)} %prepare.1.send_ref, bf16[8,128]{1,0:T(8,128)(2,1)} %pad_maximum_fusion.meta_ref), custom_call_target="tpu_custom_call" | custom-call | tf_op jit(solution)/shard_map/dispatch/pallas_call | solution.py:323
  86.5 0.7 constant_dynamic-slice_fusion
  87.2 0.7 reshape.116.mix_ref
  87.9 0.7 reshape.115.experts_ref
  88.6 7.0 %expert_in.1.x_ref = bf16[192,1024]{1,0:T(8,128)(2,1)} custom-call(bf16[4,128,8,512]{3,2,1,0:T(8,128)(2,1)} %get-tuple-element.10.rows_ref.own_ref, f32[1,2048]{1,0:T(1,128)} %bitcast.60, bf16[192,2048]{1,0:T(8,128)(2,1)} %bitcast.56, bf16[192,2048]{1,0:T(8,128)(2,1)} %bitcast.57), custom_call_target="tpu_custom_call" | custom-call | tf_op jit(solution)/shard_map/expert_in/pallas_call | solution.py:364
  95.6 14.6 %tp_gather.1 = bf16[4,192,1024]{2,1,0:T(8,128)(2,1)} custom-call(bf16[192,1024]{1,0:T(8,128)(2,1)} %expert_in.1.x_ref), custom_call_target="tpu_custom_call" | custom-call | tf_op jit(solution)/shard_map/tp_gather/pallas_call | solution.py:435
  110.2 5.4 %expert_out.1.send_ref = bf16[128,8,512]{2,1,0:T(8,128)(2,1)} custom-call(s32[128]{0:T(128)} %order_ref.1, s32[1]{0:T(128)} %bitcast.11.tp_ref, bf16[768,1024]{1,0:T(8,128)(2,1)} %bitcast.55, bf16[768,512]{1,0:T(8,128)(2,1)} %bitcast.58, bf16[4,128,8,512]{3,2,1,0:T(8,128)(2,1)} %get-tuple-element.10.rows_ref.own_ref), custom_call_target="tpu_custom_call" | custom-call | tf_op jit(solution)/shard_map/expert_out/pallas_call | solution.py:462
  115.6 43.7 %give_back.1.came_ref = bf16[128,8,512]{2,1,0:T(8,128)(2,1)} custom-call(bf16[128,8,512]{2,1,0:T(8,128)(2,1)} %expert_out.1.send_ref), custom_call_target="tpu_custom_call" | custom-call | tf_op jit(solution)/shard_map/give_back/pallas_call | solution.py:517
  159.3 2.6 %combine.1 = bf16[64,512]{1,0:T(8,128)(2,1)} custom-call(s32[64,8]{1,0:T(8,128)} %reshape.115.experts_ref, f32[64,8]{1,0:T(8,128)} %reshape.116.mix_ref, bf16[128,8,512]{2,1,0:T(8,128)(2,1)} %give_back.1.came_ref), custom_call_target="tpu_custom_call" | custom-call | tf_op jit(solution)/shard_map/combine/pallas_call | solution.py:536
  (4 shorter events, 0.1 us)
Async XLA Ops:
  0.0 11.3 %copy-start = (bf16[512,2048]{1,0:T(8,128)(2,1)S(1)}, bf16[512,2048]{1,0:T(8,128)(2,1)}, u32[]{:S(2)}) copy-start(bf16[512,2048]{1,0:T(8,128)(2,1)} %param.23) | copy-start | bytes 6291460

commit v3 on v2

--- a/solution.py
+++ b/solution.py
@@ -104,26 +104,26 @@
 
 
 def slot_matrices(experts, mix, count):
-    tokens, top = experts.shape
-    lanes = lax.broadcasted_iota(jnp.int32, (tokens, count), 1)
-    named = jnp.zeros((tokens, count), jnp.float32)
-    mixed = jnp.zeros((tokens, count), jnp.float32)
+    top, tokens = experts.shape
+    number = lax.broadcasted_iota(jnp.int32, (count, tokens), 0).astype(jnp.float32)
+    named = jnp.zeros((count, tokens), jnp.float32)
+    mixed = jnp.zeros((count, tokens), jnp.float32)
     for k in range(top):
-        hit = experts[:, k : k + 1] == lanes
+        hit = experts[k : k + 1, :] == number
         named = jnp.where(hit, 1.0, named)
-        mixed = jnp.where(hit, mix[:, k : k + 1], mixed)
+        mixed = jnp.where(hit, mix[k : k + 1, :], mixed)
     row = lax.broadcasted_iota(jnp.int32, (tokens, tokens), 0)
     col = lax.broadcasted_iota(jnp.int32, (tokens, tokens), 1)
-    earlier = jnp.where(col < row, 1.0, 0.0).astype(jnp.bfloat16)
-    rank = jnp.dot(earlier, named.astype(jnp.bfloat16), preferred_element_type=jnp.float32)
+    earlier = jnp.where(row < col, 1.0, 0.0).astype(jnp.bfloat16)
+    rank = jnp.dot(named.astype(jnp.bfloat16), earlier, preferred_element_type=jnp.float32)
     marked = jnp.where(named > 0.0, rank, 255.0).astype(jnp.bfloat16)
-    source = lax.broadcasted_iota(jnp.int32, (count, count * CAP), 0)
-    target = lax.broadcasted_iota(jnp.int32, (count, count * CAP), 1)
+    target = lax.broadcasted_iota(jnp.int32, (count * CAP, count), 0)
+    source = lax.broadcasted_iota(jnp.int32, (count * CAP, count), 1)
     spread = jnp.where(target // CAP == source, 1.0, 0.0).astype(jnp.bfloat16)
-    rank_wide = jnp.dot(marked, spread, preferred_element_type=jnp.float32)
-    mix_wide = jnp.dot(mixed.astype(jnp.bfloat16), spread, preferred_element_type=jnp.float32)
+    rank_wide = jnp.dot(spread, marked, preferred_element_type=jnp.float32)
+    mix_wide = jnp.dot(spread, mixed.astype(jnp.bfloat16), preferred_element_type=jnp.float32)
     place = lax.rem(
-        lax.broadcasted_iota(jnp.int32, (tokens, count * CAP), 1), CAP
+        lax.broadcasted_iota(jnp.int32, (count * CAP, tokens), 0), CAP
     ).astype(jnp.float32)
     chosen = rank_wide == place
     selector = jnp.where(chosen, 1.0, 0.0).astype(jnp.bfloat16)
@@ -131,25 +131,30 @@
     return selector, weighted
 
 
-def prepare_kernel(count, terms_ref, residual_ref, experts_ref, out_ref):
+def prepare_kernel(count, terms_ref, residual_ref, experts_ref, weights_ref, out_ref, meta_ref):
     total = residual_ref[...].astype(jnp.float32)
     for o in range(terms_ref.shape[0]):
         total = total + terms_ref[o].astype(jnp.float32)
     hidden = total.astype(jnp.bfloat16)
-    experts = experts_ref[...]
-    selector, _ = slot_matrices(experts, experts.astype(jnp.float32), count)
-    rows = lax.dot_general(
-        selector, hidden, (((0,), (0,)), ((), ())), preferred_element_type=jnp.float32
-    )
+    experts = experts_ref[...].astype(jnp.float32)
+    weights = weights_ref[...]
+    mix = weights / jnp.sum(weights, axis=0, keepdims=True)
+    selector, _ = slot_matrices(experts, mix, count)
+    rows = jnp.dot(selector, hidden, preferred_element_type=jnp.float32)
     out_ref[...] = rows.reshape(out_ref.shape).astype(jnp.bfloat16)
-
-
-def prepare(terms, residual, experts, count):
+    meta_ref[...] = jnp.zeros_like(meta_ref)
+    meta_ref[:, : experts.shape[1]] = jnp.concatenate([experts, mix], axis=0).astype(jnp.bfloat16)
+
+
+def prepare(terms, residual, experts, weights, count):
     return pl.pallas_call(
         functools.partial(prepare_kernel, count),
-        out_shape=jax.ShapeDtypeStruct((count, CAP, residual.shape[1]), jnp.bfloat16),
+        out_shape=(
+            jax.ShapeDtypeStruct((count, CAP, residual.shape[1]), jnp.bfloat16),
+            jax.ShapeDtypeStruct((2 * experts.shape[0], 128), jnp.bfloat16),
+        ),
         name="prepare",
-    )(terms, residual, experts)
+    )(terms, residual, experts, weights)
 
 
 def dispatch_kernel(
@@ -336,66 +341,82 @@
     )(send, meta)
 
 
-def expert_in_kernel(rows_ref, gain_ref, gate_ref, up_ref, out_ref):
-    parts, sources, cap, width = rows_ref.shape
-    rows = sources * cap
-    total = parts * width
-    wide = [rows_ref[p].astype(jnp.float32).reshape(rows, width) for p in range(parts)]
-    squares = sum(jnp.sum(part * part, axis=1, keepdims=True) for part in wide)
-    factor = lax.rsqrt(squares / total + 1e-06)
-    normed = jnp.concatenate(
-        [
-            (part * factor * gain_ref[:, p * width : (p + 1) * width]).astype(jnp.bfloat16)
-            for p, part in enumerate(wide)
-        ],
-        axis=1,
-    )
-    dims = (((1,), (1,)), ((), ()))
-    gate = lax.dot_general(gate_ref[...], normed, dims, preferred_element_type=jnp.float32)
-    up = lax.dot_general(up_ref[...], normed, dims, preferred_element_type=jnp.float32)
-    out_ref[...] = (gate / (1.0 + jnp.exp(-gate)) * up).astype(jnp.bfloat16)
-
-
-def expert_in(full, gain, gate, up):
-    parts, sources, cap, width = full.shape
-    tiles = 4 if sources >= 64 else 1
-    part_rows = sources // tiles
-    ff = gate.shape[0]
-    return pl.pallas_call(
-        expert_in_kernel,
-        grid=(tiles,),
-        out_shape=jax.ShapeDtypeStruct((ff, sources * cap), jnp.bfloat16),
-        in_specs=[
-            pl.BlockSpec((parts, part_rows, cap, width), lambda i: (0, i, 0, 0)),
-            pl.BlockSpec((1, gain.shape[1]), lambda i: (0, 0)),
-            pl.BlockSpec(gate.shape, lambda i: (0, 0)),
-            pl.BlockSpec(up.shape, lambda i: (0, 0)),
-        ],
-        out_specs=pl.BlockSpec((ff, part_rows * cap), lambda i: (0, i)),
-        name="expert_in",
-    )(full, gain, gate, up)
-
-
-def gather_kernel(tps, chunks, x_ref, out_ref, own_sem, send_sem, recv_sem, relay_send, relay_recv):
+def experts_kernel(
+    eps,
+    tps,
+    tiles,
+    inverse_ref,
+    full_ref,
+    gain_ref,
+    gate_ref,
+    up_ref,
+    down_ref,
+    came_ref,
+    act_ref,
+    value_ref,
+    back_ref,
+    send_sem,
+    recv_sem,
+    relay_send,
+    relay_recv,
+    own_sem,
+    back_send,
+    back_recv,
+):
+    ep = lax.axis_index("ep")
     tp = lax.axis_index("tp")
     right = lax.rem(tp + 1, tps)
     left = lax.rem(tp + tps - 1, tps)
     sides = (right, left)
+    parts, sources, cap, width = full_ref.shape
+    chunk = sources // tiles
+    rows = chunk * cap
+    ff = act_ref.shape[1]
     barrier = pltpu.get_barrier_semaphore()
+
+    def greet(k, carry):
+        pl.semaphore_signal(
+            barrier, inc=1, device_id={"ep": lax.rem(ep + k, eps)}, device_id_type=MESH
+        )
+        return carry
+
     for side in sides:
         pl.semaphore_signal(barrier, inc=1, device_id={"tp": side}, device_id_type=MESH)
-    own = pltpu.make_async_copy(x_ref, out_ref.at[tp], own_sem)
-    own.start()
-    pl.semaphore_wait(barrier, 2)
-    size = x_ref.shape[0] // chunks
+    lax.fori_loop(1, eps, greet, 0)
+
+    def span(i):
+        return pl.ds(i * rows if isinstance(i, int) else pl.multiple_of(i * rows, rows), rows)
+
+    def enter(i, carry):
+        wide = [
+            full_ref[p, pl.ds(i * chunk, chunk)].astype(jnp.float32).reshape(rows, width)
+            for p in range(parts)
+        ]
+        squares = sum(jnp.sum(part * part, axis=1, keepdims=True) for part in wide)
+        factor = lax.rsqrt(squares / (parts * width) + 1e-06)
+        normed = jnp.concatenate(
+            [
+                (part * factor * gain_ref[:, p * width : (p + 1) * width]).astype(jnp.bfloat16)
+                for p, part in enumerate(wide)
+            ],
+            axis=1,
+        )
+        dims = (((1,), (1,)), ((), ()))
+        gate = lax.dot_general(gate_ref[...], normed, dims, preferred_element_type=jnp.float32)
+        up = lax.dot_general(up_ref[...], normed, dims, preferred_element_type=jnp.float32)
+        act_ref[tp, :, span(i)] = (gate / (1.0 + jnp.exp(-gate)) * up).astype(jnp.bfloat16)
+        return carry
+
+    lax.fori_loop(0, tiles, enter, 0)
+    pl.semaphore_wait(barrier, eps + 1)
     copies = []
-    for c in range(chunks):
-        part = pl.ds(c * size, size)
+    for c in range(tiles):
         pair = []
         for way in range(2):
+            block = act_ref.at[tp, :, span(c)]
             copy = pltpu.make_async_remote_copy(
-                src_ref=x_ref.at[part],
-                dst_ref=out_ref.at[tp, part],
+                src_ref=block,
+                dst_ref=block,
                 send_sem=send_sem.at[way, c],
                 recv_sem=recv_sem.at[way, c],
                 device_id={"tp": sides[way]},
@@ -405,12 +426,11 @@
             pair.append(copy)
         copies.append(pair)
     relays = []
-    for c in range(chunks):
-        part = pl.ds(c * size, size)
+    for c in range(tiles):
         way = c % 2
         for pair in copies[c]:
             pair.wait_recv()
-        block = out_ref.at[(left, right)[way], part]
+        block = act_ref.at[(left, right)[way], :, span(c)]
         copy = pltpu.make_async_remote_copy(
             src_ref=block,
             dst_ref=block,
@@ -421,123 +441,102 @@
         )
         copy.start()
         relays.append(copy)
-    own.wait()
+    for c in range(tiles):
+        relays[c].wait_recv()
+        act = jnp.concatenate([act_ref[p, :, span(c)] for p in range(parts)], axis=0)
+        value = lax.dot_general(
+            act, down_ref[...], (((0,), (0,)), ((), ())), preferred_element_type=jnp.float32
+        )
+        part = pl.ds(c * chunk, chunk)
+        value = value.reshape(chunk, cap, width) + full_ref[tp, part].astype(jnp.float32)
+        value_ref[part] = value.astype(jnp.bfloat16)
+
+    def place(d, carry):
+        back_ref[d] = value_ref[inverse_ref[d]]
+        return carry
+
+    lax.fori_loop(0, eps, place, 0)
+
+    def post(k, carry):
+        dst = lax.rem(ep + lax.rem(k * STRIDE, eps), eps)
+        pltpu.make_async_remote_copy(
+            src_ref=back_ref.at[dst],
+            dst_ref=came_ref.at[ep],
+            send_sem=back_send,
+            recv_sem=back_recv,
+            device_id={"ep": dst},
+            device_id_type=MESH,
+        ).start()
+        return carry
+
+    lax.fori_loop(1, eps, post, 0)
+    own = pltpu.make_async_copy(back_ref.at[ep], came_ref.at[ep], own_sem)
+    own.start()
     for pair in copies:
         for copy in pair:
             copy.wait_send()
     for copy in relays:
-        copy.wait()
-
-
-def gather(x, tps):
-    chunks = 4 if x.shape[0] % 64 == 0 else 2
+        copy.wait_send()
+    own.wait()
+    most = back_ref.at[pl.ds(0, eps - 1)]
+    pltpu.make_async_copy(most, most, back_send).wait()
+    pltpu.make_async_copy(most, most, back_recv).wait()
+
+
+def experts(inverse, full, gain, gate, up, down, eps, tps):
+    parts, sources, cap, width = full.shape
+    tiles = 4 if sources >= 64 else 2
     dma = pltpu.SemaphoreType.DMA
+    vmem = pl.BlockSpec(memory_space=pltpu.VMEM)
+    block = (sources, cap, width)
     return pl.pallas_call(
-        functools.partial(gather_kernel, tps, chunks),
-        out_shape=jax.ShapeDtypeStruct((tps,) + x.shape, x.dtype),
-        in_specs=[pl.BlockSpec(memory_space=pltpu.VMEM)],
-        out_specs=pl.BlockSpec(memory_space=pltpu.VMEM),
-        scratch_shapes=[dma, dma((2, chunks)), dma((2, chunks)), dma((chunks,)), dma((chunks,))],
+        functools.partial(experts_kernel, eps, tps, tiles),
+        out_shape=jax.ShapeDtypeStruct(block, jnp.bfloat16),
+        in_specs=[pl.BlockSpec(memory_space=pltpu.SMEM)] + [vmem] * 5,
+        out_specs=vmem,
+        scratch_shapes=[
+            pltpu.VMEM((parts, gate.shape[0], sources * cap), jnp.bfloat16),
+            pltpu.VMEM(block, jnp.bfloat16),
+            pltpu.VMEM(block, jnp.bfloat16),
+            dma((2, tiles)),
+            dma((2, tiles)),
+            dma((tiles,)),
+            dma((tiles,)),
+            dma,
+            dma,
+            dma,
+        ],
         compiler_params=pltpu.CompilerParams(collective_id=2, has_side_effects=True),
-        name="tp_gather",
-    )(x)
-
-
-def expert_out_kernel(order_ref, act_ref, down_ref, own_ref, out_ref):
-    sources, cap, width = own_ref.shape
-    base = pl.program_id(0) * sources
-    value = lax.dot_general(
-        act_ref[...], down_ref[...], (((0,), (0,)), ((), ())), preferred_element_type=jnp.float32
-    )
-    value = value.reshape(sources, cap, width) + own_ref[...].astype(jnp.float32)
-    value = value.astype(jnp.bfloat16)
-    for j in range(sources):
-        out_ref[order_ref[base + j]] = value[j]
-
-
-def expert_out(order, act, down, full, tp):
-    parts, sources, cap, width = full.shape
-    tiles = 4 if sources >= 64 else 1
-    part_rows = sources // tiles
+        name="experts",
+    )(inverse, full, gain, gate, up, down)
+
+
+def combine_kernel(tokens, inverse_ref, ep_ref, meta_ref, came_ref, out_ref):
+    count, cap, width = came_ref.shape
+    meta = meta_ref[...].astype(jnp.float32)
+    top = meta.shape[0] // 2
+    _, weighted = slot_matrices(meta[:top, :tokens], meta[top:, :tokens], count)
+    rows = came_ref[...].astype(jnp.float32).reshape(count * cap, width).astype(jnp.bfloat16)
+    out_ref[...] = lax.dot_general(
+        weighted, rows, (((0,), (0,)), ((), ())), preferred_element_type=jnp.float32
+    ).astype(jnp.bfloat16)
+
+
+def combine(inverse, ep, metas, came, tokens):
     return pl.pallas_call(
-        lambda order_ref, tp_ref, act_ref, down_ref, own_ref, out_ref: expert_out_kernel(
-            order_ref, act_ref, down_ref, own_ref, out_ref
-        ),
+        functools.partial(combine_kernel, tokens),
         grid_spec=pltpu.PrefetchScalarGridSpec(
             num_scalar_prefetch=2,
-            grid=(tiles,),
+            grid=(1,),
             in_specs=[
-                pl.BlockSpec((act.shape[0], part_rows * cap), lambda i, o, t: (0, i)),
-                pl.BlockSpec(down.shape, lambda i, o, t: (0, 0)),
-                pl.BlockSpec((None, part_rows, cap, width), lambda i, o, t: (t[0], i, 0, 0)),
+                pl.BlockSpec((None,) + metas.shape[1:], lambda i, v, e: (v[e[0]], 0, 0)),
+                pl.BlockSpec(came.shape, lambda i, v, e: (0, 0, 0)),
             ],
-            out_specs=pl.BlockSpec((sources, cap, width), lambda i, o, t: (0, 0, 0)),
+            out_specs=pl.BlockSpec((tokens, came.shape[2]), lambda i, v, e: (0, 0)),
         ),
-        out_shape=jax.ShapeDtypeStruct((sources, cap, width), jnp.bfloat16),
-        name="expert_out",
-    )(order, tp, act, down, full)
-
-
-def give_back_kernel(eps, send_ref, came_ref, own_sem, send_sem, recv_sem):
-    ep = lax.axis_index("ep")
-    barrier = pltpu.get_barrier_semaphore()
-
-    def greet(k, carry):
-        pl.semaphore_signal(
-            barrier, inc=1, device_id={"ep": lax.rem(ep + k, eps)}, device_id_type=MESH
-        )
-        return carry
-
-    lax.fori_loop(1, eps, greet, 0)
-    own = pltpu.make_async_copy(send_ref.at[ep], came_ref.at[ep], own_sem)
-    own.start()
-    pl.semaphore_wait(barrier, eps - 1)
-
-    def post(k, carry):
-        dst = lax.rem(ep + lax.rem(k * STRIDE, eps), eps)
-        pltpu.make_async_remote_copy(
-            src_ref=send_ref.at[dst],
-            dst_ref=came_ref.at[ep],
-            send_sem=send_sem,
-            recv_sem=recv_sem,
-            device_id={"ep": dst},
-            device_id_type=MESH,
-        ).start()
-        return carry
-
-    lax.fori_loop(1, eps, post, 0)
-    own.wait()
-    most = send_ref.at[pl.ds(0, eps - 1)]
-    pltpu.make_async_copy(most, most, send_sem).wait()
-    pltpu.make_async_copy(most, most, recv_sem).wait()
-
-
-def give_back(send, eps):
-    dma = pltpu.SemaphoreType.DMA
-    return pl.pallas_call(
-        functools.partial(give_back_kernel, eps),
-        out_shape=jax.ShapeDtypeStruct(send.shape, send.dtype),
-        in_specs=[pl.BlockSpec(memory_space=pl.ANY)],
-        out_specs=pl.BlockSpec(memory_space=pl.ANY),
-        scratch_shapes=[dma, dma, dma],
-        compiler_params=pltpu.CompilerParams(collective_id=3, has_side_effects=True),
-        name="give_back",
-    )(send)
-
-
-def combine_kernel(experts_ref, mix_ref, came_ref, out_ref):
-    count, cap, width = came_ref.shape
-    _, weighted = slot_matrices(experts_ref[...], mix_ref[...], count)
-    rows = came_ref[...].astype(jnp.float32).reshape(count * cap, width).astype(jnp.bfloat16)
-    out_ref[...] = jnp.dot(weighted, rows, preferred_element_type=jnp.float32).astype(jnp.bfloat16)
-
-
-def combine(experts, mix, came):
-    return pl.pallas_call(
-        combine_kernel,
-        out_shape=jax.ShapeDtypeStruct((experts.shape[0], came.shape[2]), jnp.bfloat16),
+        out_shape=jax.ShapeDtypeStruct((tokens, came.shape[2]), jnp.bfloat16),
         name="combine",
-    )(experts, mix, came)
+    )(inverse, ep, metas, came)
 
 
 def shards(
@@ -560,30 +559,21 @@
     tps = lax.axis_size("tp")
     eps = lax.axis_size("ep")
     ep = lax.axis_index("ep")
-    tp = lax.axis_index("tp")
     context = attention_block(
         queries, new_keys, new_values, key_cache, value_cache, cache_lengths, KVHEADS // tps
     )
     head_terms = jnp.dot(context, out_weight, preferred_element_type=jnp.float32)
     terms = exchange(head_terms.astype(jnp.bfloat16), tps)
-    tokens, top = route_experts.shape
-    mixing = (route_weights / jnp.sum(route_weights, axis=1, keepdims=True)).astype(jnp.bfloat16)
-    meta = jnp.concatenate(
-        [route_experts.astype(jnp.bfloat16).reshape(-1), mixing.reshape(-1)]
-    )
-    pairs = tokens * top
-    meta = jnp.pad(meta, (0, -(2 * pairs) % 1024)).reshape(-1, 128)
-    send = prepare(terms, residual, route_experts, eps)
+    places = jnp.arange(eps, dtype=jnp.int32)
+    inverse = jnp.sum(
+        jnp.where(request_order[None, :] == places[:, None], places[None, :], 0), axis=1
+    )
+    send, meta = prepare(terms, residual, route_experts.T, route_weights.T, eps)
     full, metas = dispatch(send, meta, eps, tps)
-    act = expert_in(full, norm_gain[None, :], expert_gate[0].T, expert_up[0].T)
-    act_full = gather(act, tps).reshape(-1, act.shape[1])
-    back = expert_out(request_order, act_full, expert_down[0], full, tp[None].astype(jnp.int32))
-    came = give_back(back, eps)
-    origin = jnp.argmax(request_order == ep).astype(jnp.int32)
-    theirs = lax.dynamic_index_in_dim(metas, origin, 0, keepdims=False).reshape(-1)
-    their_experts = theirs[:pairs].reshape(tokens, top).astype(jnp.int32)
-    their_mix = theirs[pairs : 2 * pairs].reshape(tokens, top).astype(jnp.float32)
-    return combine(their_experts, their_mix, came)
+    came = experts(
+        inverse, full, norm_gain[None, :], expert_gate[0].T, expert_up[0].T, expert_down[0], eps, tps
+    )
+    return combine(inverse, ep[None].astype(jnp.int32), metas, came, route_experts.shape[0])
 
 
 def solution(mesh):

time: 163 us -> 148 us (0.908)
  Pallas kernels: 147 us -> 142 us
  local copies, waits for them, and re-layouts: 3.91 us -> 0.06 us
  other arithmetic: 4.41 us -> 1.02 us
  between operations: 2.56 us -> 0.9 us
    pallas_call x6 -> x3, Pallas kernels: 76.2 us -> 69.4 us  [the longest x1 63.6 us: experts(): pl.pallas_call(functools.partial(experts_kernel, eps, tps, tiles), out_sh...]
    pallas_call x1, Pallas kernels: 61.9 us -> 63.6 us  [dispatch(): pl.pallas_call(functools.partial(dispatch_kernel, eps, tps), out_shape=(j...]
where the time goes in v3:
time: 148 us
  Pallas kernels  142 us (96%)
  matrix products  3.71 us (3%)
    pallas_call x1, Pallas kernels, dispatch(): pl.pallas_call(functools.partial(dispatch_kernel, eps, tps), out_shape=(j...  63.6 us
    pallas_call x1, Pallas kernels, experts(): pl.pallas_call(functools.partial(experts_kernel, eps, tps, tiles), out_sh...  63.6 us
    pallas_call x1, Pallas kernels, exchange(): pl.pallas_call(functools.partial(exchange_kernel, tps), out_shape=jax.Sha...  9.22 us
    pallas_call x1, Pallas kernels, combine(): pl.pallas_call(functools.partial(combine_kernel, tokens), grid_spec=pltpu...  3.16 us

profile of v3, /device:TPU:1, one launch (start us, length us, event | category | flops | bytes accessed | tf_op | source)
XLA Modules:
  0.0 148.0 jit_solution(10292813465592350273)
XLA Ops:
  0.0 0.0 copy-start
  0.9 1.3 select_reduce_fusion
  2.2 0.3 fusion.4
  2.4 1.2 fusion.3
  3.7 0.1 copy.20
  3.7 0.0 copy-done
  3.8 0.0 copy-start.1
  3.8 1.2 convolution_convert_fusion.x_ref
  5.0 9.2 %tp_exchange.1.terms_ref = bf16[4,64,512]{2,1,0:T(8,128)(2,1)} custom-call(bf16[64,2048]{1,0:T(8,128)(2,1)} %convolution_convert_fusion.x_ref), custom_call_target="tpu_custom_call" | custom-call | tf_op jit(solution)/shard_map/tp_exchange/pallas_call | solution.py:91
  14.2 2.7 %prepare.1 = (bf16[128,8,512]{2,1,0:T(8,128)(2,1)}, bf16[16,128]{1,0:T(8,128)(2,1)}) custom-call(bf16[4,64,512]{2,1,0:T(8,128)(2,1)} %tp_exchange.1.terms_ref, bf16[64,512]{1,0:T(8,128)(2,1)} %residual_ref.1, s32[8,64]{1,0:T(8,128)} %bitcast.61, f32[8,64]{1,0:T(8,128)} %bitcast.62), custom_call_target="tpu_custom_call" | custom-call | tf_op jit(solution)/shard_map/prepare/pallas_call | solution.py:150
  16.9 63.6 %dispatch.1 = (bf16[4,128,8,512]{3,2,1,0:T(8,128)(2,1)}, bf16[128,16,128]{2,1,0:T(8,128)(2,1)}) custom-call(bf16[128,8,512]{2,1,0:T(8,128)(2,1)} %get-tuple-element.9.send_ref, bf16[16,128]{1,0:T(8,128)(2,1)} %get-tuple-element.10.meta_ref), custom_call_target="tpu_custom_call" | custom-call | tf_op jit(solution)/shard_map/dispatch/pallas_call | solution.py:328
  80.5 0.0 copy-done.1
  80.5 0.7 select_reduce_fusion.1.inverse_ref
  81.2 63.6 %experts.1.came_ref = bf16[128,8,512]{2,1,0:T(8,128)(2,1)} custom-call(s32[128]{0:T(128)} %select_reduce_fusion.1.inverse_ref, bf16[4,128,8,512]{3,2,1,0:T(8,128)(2,1)} %get-tuple-element.12.full_ref, f32[1,2048]{1,0:T(1,128)} %bitcast.60, bf16[192,2048]{1,0:T(8,128)(2,1)} %bitcast.56, bf16[192,2048]{1,0:T(8,128)(2,1)} %bitcast.57, bf16[768,512]{1,0:T(8,128)(2,1)} %bitcast.58), custom_call_target="tpu_custom_call" | custom-call | tf_op jit(solution)/shard_map/experts/pallas_call | solution.py:492
  144.8 3.2 %combine.1 = bf16[64,512]{1,0:T(8,128)(2,1)} custom-call(s32[128]{0:T(128)} %select_reduce_fusion.1.inverse_ref, s32[1]{0:T(128)} %bitcast.ep_ref, bf16[128,16,128]{2,1,0:T(8,128)(2,1)} %get-tuple-element.11.meta_ref, bf16[128,8,512]{2,1,0:T(8,128)(2,1)} %experts.1.came_ref), custom_call_target="tpu_custom_call" | custom-call | tf_op jit(solution)/shard_map/combine/pallas_call | solution.py:526
  (3 shorter events, 0.0 us)
Async XLA Ops:
  0.0 3.7 %copy-start = (bf16[512,2048]{1,0:T(8,128)(2,1)S(1)}, bf16[512,2048]{1,0:T(8,128)(2,1)}, u32[]{:S(2)}) copy-start(bf16[512,2048]{1,0:T(8,128)(2,1)} %param.23) | copy-start | bytes 6291460
  3.8 76.7 %copy-start.1 = (s32[128]{0:T(128)S(1)}, s32[128]{0:T(128)}, u32[]{:S(2)}) copy-start(s32[128]{0:T(128)} %param.21) | copy-start | bytes 1540

commit v4 on v3

v4 whole, which is shorter than its diff:
```python
import functools
import math

import jax
import jax.numpy as jnp
from jax import lax
from jax.experimental import pallas as pl
from jax.experimental.pallas import tpu as pltpu
from jax.sharding import PartitionSpec as P

HEAD = 128
QHEADS = 16
KVHEADS = 4
CAP = 8
STRIDE = 37
LAG = 32
AHEAD = 48
MESH = pl.DeviceIdType.MESH


def attention_block(queries, new_keys, new_values, key_cache, value_cache, cache_lengths, kv_local):
    tokens_here = queries.shape[0]
    cached = key_cache.shape[1]
    group_size = QHEADS // KVHEADS
    query_view = queries.reshape(tokens_here, kv_local, group_size, HEAD)
    all_keys = jnp.concatenate([key_cache[0], new_keys], axis=0).reshape(
        cached + tokens_here, kv_local, HEAD
    )
    all_values = jnp.concatenate([value_cache[0], new_values], axis=0).reshape(
        cached + tokens_here, kv_local, HEAD
    )
    scores = jnp.einsum(
        "tghd,kgd->tghk", query_view, all_keys, preferred_element_type=jnp.float32
    ) / math.sqrt(HEAD)
    position = jnp.arange(cached + tokens_here, dtype=jnp.int32)
    current = jnp.arange(tokens_here, dtype=jnp.int32)
    visible = jnp.where(
        position[None, :] < cached,
        position[None, :] < cache_lengths[0],
        position[None, :] - cached <= current[:, None],
    )
    visible = visible[:, None, None, :]
    highest = jnp.max(jnp.where(visible, scores, -1e30), axis=-1, keepdims=True)
    raised = jnp.exp(jnp.where(visible, scores - highest, -1e30))
    totals = jnp.sum(raised, axis=-1, keepdims=True)
    weights = raised.astype(jnp.bfloat16)
    context = (
        jnp.einsum("tghk,kgd->tghd", weights, all_values, preferred_element_type=jnp.float32)
        / totals
    )
    return context.astype(jnp.bfloat16).reshape(tokens_here, -1)


def row_span(eps):
    return 16 if eps > 16 else 2


def slot_matrices(experts, mix, count):
    top, tokens = experts.shape
    number = lax.broadcasted_iota(jnp.int32, (count, tokens), 0).astype(jnp.float32)
    named = jnp.zeros((count, tokens), jnp.float32)
    mixed = jnp.zeros((count, tokens), jnp.float32)
    for k in range(top):
        hit = experts[k : k + 1, :] == number
        named = jnp.where(hit, 1.0, named)
        mixed = jnp.where(hit, mix[k : k + 1, :], mixed)
    row = lax.broadcasted_iota(jnp.int32, (tokens, tokens), 0)
    col = lax.broadcasted_iota(jnp.int32, (tokens, tokens), 1)
    earlier = jnp.where(row < col, 1.0, 0.0).astype(jnp.bfloat16)
    rank = jnp.dot(named.astype(jnp.bfloat16), earlier, preferred_element_type=jnp.float32)
    marked = jnp.where(named > 0.0, rank, 255.0).astype(jnp.bfloat16)
    target = lax.broadcasted_iota(jnp.int32, (count * CAP, count), 0)
    source = lax.broadcasted_iota(jnp.int32, (count * CAP, count), 1)
    spread = jnp.where(target // CAP == source, 1.0, 0.0).astype(jnp.bfloat16)
    rank_wide = jnp.dot(spread, marked, preferred_element_type=jnp.float32)
    mix_wide = jnp.dot(spread, mixed.astype(jnp.bfloat16), preferred_element_type=jnp.float32)
    place = lax.rem(
        lax.broadcasted_iota(jnp.int32, (count * CAP, tokens), 0), CAP
    ).astype(jnp.float32)
    chosen = rank_wide == place
    selector = jnp.where(chosen, 1.0, 0.0).astype(jnp.bfloat16)
    weighted = jnp.where(chosen, mix_wide, 0.0).astype(jnp.bfloat16)
    return selector, weighted


def layer_kernel(eps, tps, tiles, *refs):
    (
        inverse_ref,
        terms_ref,
        residual_ref,
        experts_ref,
        weights_ref,
        gain_ref,
        gate_ref,
        up_ref,
        down_ref,
        out_ref,
        got_ref,
        send_ref,
        meta_ref,
        full_ref,
        metas_ref,
        act_ref,
        value_ref,
        back_ref,
        came_ref,
        own_sem,
        term_send,
        term_recv,
        send_sem,
        meta_send,
        meta_recv,
        recv_sem,
        right_send,
        left_send,
        left_recv,
        right_recv,
        relay_send,
        relay_recv,
        act_send,
        act_recv,
        act_relay_send,
        act_relay_recv,
        back_send,
        back_recv,
    ) = refs
    ep = lax.axis_index("ep")
    tp = lax.axis_index("tp")
    right = lax.rem(tp + 1, tps)
    left = lax.rem(tp + tps - 1, tps)
    sides = (right, left)
    tokens, features = residual_ref.shape
    top = experts_ref.shape[0]
    barrier = pltpu.get_barrier_semaphore()

    def greet(k, carry):
        pl.semaphore_signal(
            barrier, inc=1, device_id={"ep": lax.rem(ep + k, eps)}, device_id_type=MESH
        )
        return carry

    for o in range(1, tps):
        pl.semaphore_signal(
            barrier, inc=1, device_id={"tp": lax.rem(tp + o, tps)}, device_id_type=MESH
        )
    lax.fori_loop(1, eps, greet, 0)

    def columns(p):
        return terms_ref.at[:, pl.ds(pl.multiple_of(p * features, features), features)]

    own_terms = pltpu.make_async_copy(columns(tp), got_ref.at[0], own_sem.at[0])
    own_terms.start()
    named = experts_ref[...].astype(jnp.float32)
    weights = weights_ref[...]
    mix = weights / jnp.sum(weights, axis=0, keepdims=True)
    meta_ref[...] = jnp.zeros_like(meta_ref)
    meta_ref[:, :tokens] = jnp.concatenate([named, mix], axis=0).astype(jnp.bfloat16)
    selector, _ = slot_matrices(named, mix, eps)
    pl.semaphore_wait(barrier, eps + tps - 2)
    exchanged = []
    for o in range(1, tps):
        peer = lax.rem(tp + o, tps)
        copy = pltpu.make_async_remote_copy(
            src_ref=columns(peer),
            dst_ref=got_ref.at[o],
            send_sem=term_send.at[o - 1],
            recv_sem=term_recv.at[o - 1],
            device_id={"tp": peer},
            device_id_type=MESH,
        )
        copy.start()
        exchanged.append(copy)
    own_terms.wait()
    for copy in exchanged:
        copy.wait()
    total = residual_ref[...].astype(jnp.float32)
    for o in range(tps):
        total = total + got_ref[o].astype(jnp.float32)
    picked = jnp.dot(selector, total.astype(jnp.bfloat16), preferred_element_type=jnp.float32)
    send_ref[...] = picked.reshape(send_ref.shape).astype(jnp.bfloat16)
    own = pltpu.make_async_copy(send_ref.at[ep], full_ref.at[tp, ep], recv_sem.at[0])
    own.start()
    own_meta = pltpu.make_async_copy(meta_ref, metas_ref.at[ep], own_sem.at[1])
    own_meta.start()
    wide = row_span(eps)
    rows = eps // wide
    row = lax.div(ep, wide)
    place = lax.rem(ep, wide)

    def offset(k):
        return lax.rem(k * STRIDE, eps)

    def source(k):
        return lax.rem(ep + eps - offset(k), eps)

    def post(k):
        off = offset(k)
        dst = lax.rem(ep + off, eps)
        pltpu.make_async_remote_copy(
            src_ref=send_ref.at[dst],
            dst_ref=full_ref.at[tp, ep],
            send_sem=send_sem,
            recv_sem=recv_sem.at[off],
            device_id={"ep": dst},
            device_id_type=MESH,
        ).start()

    def meta_near(k, carry):
        pltpu.make_async_remote_copy(
            src_ref=meta_ref,
            dst_ref=metas_ref.at[ep],
            send_sem=meta_send.at[0],
            recv_sem=meta_recv.at[0],
            device_id={"ep": row * wide + lax.rem(place + k, wide)},
            device_id_type=MESH,
        ).start()
        return carry

    def meta_far(k, carry):
        ours = metas_ref.at[pl.ds(row * wide, wide)]
        pltpu.make_async_remote_copy(
            src_ref=ours,
            dst_ref=ours,
            send_sem=meta_send.at[1],
            recv_sem=meta_recv.at[1],
            device_id={"ep": lax.rem(row + k, rows) * wide + place},
            device_id_type=MESH,
        ).start()
        return carry

    def spread(k):
        block = full_ref.at[tp, source(k)]
        pltpu.make_async_copy(block, block, recv_sem.at[offset(k)]).wait()
        for side, ssem, rsem in ((right, right_send, left_recv), (left, left_send, right_recv)):
            pltpu.make_async_remote_copy(
                src_ref=block,
                dst_ref=block,
                send_sem=ssem,
                recv_sem=rsem.at[k],
                device_id={"tp": side},
                device_id_type=MESH,
            ).start()

    def relay(k, way):
        src = source(k)
        from_left = full_ref.at[left, src]
        from_right = full_ref.at[right, src]
        pltpu.make_async_copy(from_left, from_left, left_recv.at[k]).wait()
        pltpu.make_async_copy(from_right, from_right, right_recv.at[k]).wait()
        block, side = ((from_left, right), (from_right, left))[way]
        pltpu.make_async_remote_copy(
            src_ref=block,
            dst_ref=block,
            send_sem=relay_send.at[way],
            recv_sem=relay_recv.at[way],
            device_id={"tp": side},
            device_id_type=MESH,
        ).start()

    def drain(ref, sem):
        pltpu.make_async_copy(ref, ref, sem).wait()

    def pairs(low, high, step):
        def both(i, carry):
            for way in range(2):
                step(2 * i + way, way)
            return carry

        lax.fori_loop(low // 2, high // 2, both, 0)

    def first(k, carry):
        post(k)
        return carry

    def opening(k, way):
        post(k + ahead)
        spread(k)

    def middle(k, way):
        post(k + ahead)
        spread(k)
        relay(k - lag, way)

    def closing(k, way):
        spread(k)
        relay(k - lag, way)

    ahead, lag = min(AHEAD, eps // 2), min(LAG, eps // 2)
    lax.fori_loop(1, ahead, first, 0)
    lax.fori_loop(1, wide, meta_near, 0)
    pairs(0, lag, opening)
    pairs(lag, eps - ahead, middle)
    own_meta.wait()
    near = metas_ref.at[pl.ds(0, wide - 1)]
    drain(near, meta_recv.at[0])
    lax.fori_loop(1, rows, meta_far, 0)
    pairs(eps - ahead, eps, closing)
    pairs(eps - lag, eps, relay)
    drain(near, meta_send.at[0])
    far = metas_ref.at[pl.ds(0, (rows - 1) * wide)]
    drain(far, meta_send.at[1])
    drain(far, meta_recv.at[1])
    drain(send_ref.at[pl.ds(0, eps - 1)], send_sem)
    drain(send_ref, right_send)
    drain(send_ref, left_send)
    half = send_ref.at[pl.ds(0, eps // 2)]
    for way in range(2):
        drain(half, relay_send.at[way])
        drain(half, relay_recv.at[way])

    parts, sources, cap, width = full_ref.shape
    chunk = sources // tiles
    rows = chunk * cap
    ff = act_ref.shape[1]
    def span(i):
        return pl.ds(i * rows if isinstance(i, int) else pl.multiple_of(i * rows, rows), rows)

    def enter(i, carry):
        wide = [
            full_ref[p, pl.ds(i * chunk, chunk)].astype(jnp.float32).reshape(rows, width)
            for p in range(parts)
        ]
        squares = sum(jnp.sum(part * part, axis=1, keepdims=True) for part in wide)
        factor = lax.rsqrt(squares / (parts * width) + 1e-06)
        normed = jnp.concatenate(
            [
                (part * factor * gain_ref[:, p * width : (p + 1) * width]).astype(jnp.bfloat16)
                for p, part in enumerate(wide)
            ],
            axis=1,
        )
        dims = (((1,), (1,)), ((), ()))
        gate = lax.dot_general(gate_ref[...], normed, dims, preferred_element_type=jnp.float32)
        up = lax.dot_general(up_ref[...], normed, dims, preferred_element_type=jnp.float32)
        act_ref[tp, :, span(i)] = (gate / (1.0 + jnp.exp(-gate)) * up).astype(jnp.bfloat16)
        return carry

    lax.fori_loop(0, tiles, enter, 0)
    copies = []
    for c in range(tiles):
        pair = []
        for way in range(2):
            block = act_ref.at[tp, :, span(c)]
            copy = pltpu.make_async_remote_copy(
                src_ref=block,
                dst_ref=block,
                send_sem=act_send.at[way, c],
                recv_sem=act_recv.at[way, c],
                device_id={"tp": sides[way]},
                device_id_type=MESH,
            )
            copy.start()
            pair.append(copy)
        copies.append(pair)
    relays = []
    for c in range(tiles):
        way = c % 2
        for pair in copies[c]:
            pair.wait_recv()
        block = act_ref.at[(left, right)[way], :, span(c)]
        copy = pltpu.make_async_remote_copy(
            src_ref=block,
            dst_ref=block,
            send_sem=act_relay_send.at[c],
            recv_sem=act_relay_recv.at[c],
            device_id={"tp": sides[way]},
            device_id_type=MESH,
        )
        copy.start()
        relays.append(copy)
    for c in range(tiles):
        relays[c].wait_recv()
        act = jnp.concatenate([act_ref[p, :, span(c)] for p in range(parts)], axis=0)
        value = lax.dot_general(
            act, down_ref[...], (((0,), (0,)), ((), ())), preferred_element_type=jnp.float32
        )
        part = pl.ds(c * chunk, chunk)
        value = value.reshape(chunk, cap, width) + full_ref[tp, part].astype(jnp.float32)
        value_ref[part] = value.astype(jnp.bfloat16)

    def arrange(d, carry):
        back_ref[d] = value_ref[inverse_ref[d]]
        return carry

    lax.fori_loop(0, eps, arrange, 0)

    def post_back(k, carry):
        dst = lax.rem(ep + lax.rem(k * STRIDE, eps), eps)
        pltpu.make_async_remote_copy(
            src_ref=back_ref.at[dst],
            dst_ref=came_ref.at[ep],
            send_sem=back_send,
            recv_sem=back_recv,
            device_id={"ep": dst},
            device_id_type=MESH,
        ).start()
        return carry

    lax.fori_loop(1, eps, post_back, 0)
    own = pltpu.make_async_copy(back_ref.at[ep], came_ref.at[ep], own_sem.at[2])
    own.start()
    theirs = metas_ref[inverse_ref[ep]].astype(jnp.float32)
    _, weighted = slot_matrices(theirs[:top, :tokens], theirs[top:, :tokens], eps)
    for pair in copies:
        for copy in pair:
            copy.wait_send()
    for copy in relays:
        copy.wait_send()
    own.wait()
    most = back_ref.at[pl.ds(0, eps - 1)]
    pltpu.make_async_copy(most, most, back_send).wait()
    pltpu.make_async_copy(most, most, back_recv).wait()
    came = came_ref[...].astype(jnp.float32).reshape(eps * cap, width).astype(jnp.bfloat16)
    out_ref[...] = lax.dot_general(
        weighted, came, (((0,), (0,)), ((), ())), preferred_element_type=jnp.float32
    ).astype(jnp.bfloat16)


def layer(inverse, terms, residual, experts, weights, gain, gate, up, down, eps, tps):
    tokens, width = residual.shape
    tiles = 4 if eps >= 64 else 2
    dma = pltpu.SemaphoreType.DMA
    vmem = pl.BlockSpec(memory_space=pltpu.VMEM)
    meta = (2 * experts.shape[0], 128)

    def room(*shape):
        return pltpu.VMEM(shape, jnp.bfloat16)

    return pl.pallas_call(
        functools.partial(layer_kernel, eps, tps, tiles),
        out_shape=jax.ShapeDtypeStruct((tokens, width), jnp.bfloat16),
        in_specs=[pl.BlockSpec(memory_space=pltpu.SMEM)] + [vmem] * 8,
        out_specs=vmem,
        scratch_shapes=[
            room(tps, tokens, width),
            room(eps, CAP, width),
            room(*meta),
            room(tps, eps, CAP, width),
            room(eps, *meta),
            room(tps, gate.shape[0], eps * CAP),
            room(eps, CAP, width),
            room(eps, CAP, width),
            room(eps, CAP, width),
            dma((3,)),
            dma((tps - 1,)),
            dma((tps - 1,)),
            dma,
            dma((2,)),
            dma((2,)),
            dma((eps,)),
            dma,
            dma,
            dma((eps,)),
            dma((eps,)),
            dma((2,)),
            dma((2,)),
            dma((2, tiles)),
            dma((2, tiles)),
            dma((tiles,)),
            dma((tiles,)),
            dma,
            dma,
        ],
        compiler_params=pltpu.CompilerParams(collective_id=0, has_side_effects=True),
        name="layer",
    )(inverse, terms, residual, experts, weights, gain, gate, up, down)


def shards(
    queries,
    new_keys,
    new_values,
    key_cache,
    value_cache,
    cache_lengths,
    request_order,
    residual,
    out_weight,
    norm_gain,
    route_experts,
    route_weights,
    expert_gate,
    expert_up,
    expert_down,
):
    tps = lax.axis_size("tp")
    eps = lax.axis_size("ep")
    context = attention_block(
        queries, new_keys, new_values, key_cache, value_cache, cache_lengths, KVHEADS // tps
    )
    head_terms = jnp.dot(context, out_weight, preferred_element_type=jnp.float32)
    places = jnp.arange(eps, dtype=jnp.int32)
    inverse = jnp.sum(
        jnp.where(request_order[None, :] == places[:, None], places[None, :], 0), axis=1
    )
    return layer(
        inverse,
        head_terms.astype(jnp.bfloat16),
        residual,
        route_experts.T,
        route_weights.T,
        norm_gain[None, :],
        expert_gate[0].T,
        expert_up[0].T,
        expert_down[0],
        eps,
        tps,
    )


def solution(mesh):
    return jax.shard_map(
        shards,
        mesh=mesh,
        in_specs=(
            P("ep", "tp"),
            P("ep", "tp"),
            P("ep", "tp"),
            P("ep", None, "tp"),
            P("ep", None, "tp"),
            P("ep"),
            P(),
            P("ep", "tp"),
            P("tp", None),
            P(),
            P("ep", None),
            P("ep", None),
            P("ep", None, "tp"),
            P("ep", None, "tp"),
            P("ep", None, "tp"),
        ),
        out_specs=P("ep", "tp"),
        check_vma=False,
    )
```

time: 148 us -> 130 us (0.88)
  the two profiles are of different devices: /device:TPU:1 before, /device:TPU:48 now
where the time goes in v4:
time: 130 us
  Pallas kernels  123 us (95%)
  matrix products  3.7 us (3%)
  local copies, waits for them, and re-layouts  1.54 us (1%)
    pallas_call x1, Pallas kernels, layer(): pl.pallas_call(functools.partial(layer_kernel, eps, tps, tiles), out_shap...  123 us

profile of v4, /device:TPU:48, one launch (start us, length us, event | category | flops | bytes accessed | tf_op | source)
XLA Modules:
  0.0 130.1 jit_solution(1346610045333803981)
XLA Ops:
  0.0 0.0 copy-start
  0.9 1.3 select_reduce_fusion
  2.2 0.3 fusion.4
  2.4 0.0 copy-start.1
  2.4 1.3 fusion.3
  3.7 0.1 copy.20
  3.8 0.0 copy-done
  3.8 1.2 convolution_convert_fusion.refs_1_
  4.9 0.0 copy-done.1
  4.9 0.6 select_reduce_fusion.1.refs_0_
  5.6 123.1 %layer.1 = bf16[64,512]{1,0:T(8,128)(2,1)} custom-call(s32[128]{0:T(128)} %select_reduce_fusion.1.refs_0_, bf16[64,2048]{1,0:T(8,128)(2,1)} %convolution_convert_fusion.refs_1_, bf16[64,512]{1,0:T(8,128)(2,1)} %refs_2_.1, s32[8,64]{1,0:T(8,128)} %bitcast.60, f32[8,64]{1,0:T(8,128)} %bitcast.61, f32[1,2048]{1,0:T(1,128)} %bitcast.59, ...), custom_call_target="tpu_custom_call" | custom-call | tf_op jit(solution)/shard_map/layer/pallas_call | solution.py:429
  128.6 1.5 %copy.35 = bf16[64,512]{1,0:T(8,128)(2,1)} copy(bf16[64,512]{1,0:T(8,128)(2,1)} %layer.1) | data formatting | bytes 131072
  (3 shorter events, 0.0 us)
Async XLA Ops:
  0.0 3.8 %copy-start = (bf16[512,2048]{1,0:T(8,128)(2,1)S(1)}, bf16[512,2048]{1,0:T(8,128)(2,1)}, u32[]{:S(2)}) copy-start(bf16[512,2048]{1,0:T(8,128)(2,1)} %param.23) | copy-start | bytes 6291460
  2.4 2.5 %copy-start.1 = (s32[128]{0:T(128)S(1)}, s32[128]{0:T(128)}, u32[]{:S(2)}) copy-start(s32[128]{0:T(128)} %param.21) | copy-start | bytes 1540

commit v5 on v4

--- a/solution.py
+++ b/solution.py
@@ -335,9 +335,9 @@
         act_ref[tp, :, span(i)] = (gate / (1.0 + jnp.exp(-gate)) * up).astype(jnp.bfloat16)
         return carry
 
-    lax.fori_loop(0, tiles, enter, 0)
     copies = []
     for c in range(tiles):
+        enter(c, 0)
         pair = []
         for way in range(2):
             block = act_ref.at[tp, :, span(c)]

time: 130 us -> 127 us (0.977)
  Pallas kernels: 123 us -> 120 us
    pallas_call x1, Pallas kernels: 123 us -> 120 us  [layer(): pl.pallas_call(functools.partial(layer_kernel, eps, tps, tiles), out_shap...]
where the time goes in v5:
time: 127 us
  Pallas kernels  120 us (94%)
  matrix products  3.7 us (3%)
  local copies, waits for them, and re-layouts  1.54 us (1%)
    pallas_call x1, Pallas kernels, layer(): pl.pallas_call(functools.partial(layer_kernel, eps, tps, tiles), out_shap...  120 us

profile of v5, /device:TPU:48, one launch (start us, length us, event | category | flops | bytes accessed | tf_op | source)
XLA Modules:
  0.0 126.8 jit_solution(4517908613602378538)
XLA Ops:
  0.0 0.0 copy-start
  0.9 1.3 %select_reduce_fusion = (f32[64,4]{0,1:T(4,128)S(1)}, f32[64,1,4,576]{3,0,2,1:T(8,128)S(1)}) fusion(pred[64,576]{1,0:T(8,128)(4,1)S(1)} %fusion.11, bf16[64,128]{1,0:T(8,128)(2,1)} %param.16, bf16[512,128]{1,0:T(8,128)(2,1)} %bitcast.62, bf16[64,512]{1,0:T(8,128)(2,1)} %param.15), kind=kOutput, calls=%fused_computation.8 | convolution fusion | flops 38485760 | bytes 840704 | tf_op jit(solution)/shard_map/tghd,kgd->tghk/dot_general | solution.py:32
  2.2 0.3 fusion.4
  2.4 0.0 copy-start.1
  2.4 1.3 fusion.3
  3.7 0.1 copy.20
  3.8 0.0 copy-done
  3.8 1.2 convolution_convert_fusion.refs_1_
  4.9 0.0 copy-done.1
  4.9 0.6 select_reduce_fusion.1.refs_0_
  5.6 119.8 %layer.1 = bf16[64,512]{1,0:T(8,128)(2,1)} custom-call(s32[128]{0:T(128)} %select_reduce_fusion.1.refs_0_, bf16[64,2048]{1,0:T(8,128)(2,1)} %convolution_convert_fusion.refs_1_, bf16[64,512]{1,0:T(8,128)(2,1)} %refs_2_.1, s32[8,64]{1,0:T(8,128)} %bitcast.60, f32[8,64]{1,0:T(8,128)} %bitcast.61, f32[1,2048]{1,0:T(1,128)} %bitcast.59, ...), custom_call_target="tpu_custom_call" | custom-call | tf_op jit(solution)/shard_map/layer/pallas_call | solution.py:429
  125.4 1.5 %copy.35 = bf16[64,512]{1,0:T(8,128)(2,1)} copy(bf16[64,512]{1,0:T(8,128)(2,1)} %layer.1) | data formatting | bytes 131072
  (3 shorter events, 0.0 us)
Async XLA Ops:
  0.0 3.8 %copy-start = (bf16[512,2048]{1,0:T(8,128)(2,1)S(1)}, bf16[512,2048]{1,0:T(8,128)(2,1)}, u32[]{:S(2)}) copy-start(bf16[512,2048]{1,0:T(8,128)(2,1)} %param.23) | copy-start | bytes 6291460
  2.4 2.5 %copy-start.1 = (s32[128]{0:T(128)S(1)}, s32[128]{0:T(128)}, u32[]{:S(2)}) copy-start(s32[128]{0:T(128)} %param.21) | copy-start | bytes 1540
